TPU v7x, 128 devices: a whole 4x4x4 slice. The times are simulated.
128 devices in a mesh: site: 8 (over z, core), col: 16 (over x, y).
Axes of the slice: x: 4, y: 4, z: 4, core: 2. Of those that a mesh axis runs over, the one named last changes fastest.
Arguments:
- common_geno: bfloat16 [8192, 32768], P(('site', 'col')), may hold values from 0 to 2
- rare_values: bfloat16 [2048, 512, 256], P(('site', 'col')), may hold values from -24 to 24
- block_tile: int32 [2048], P(('site', 'col')), may hold values from 0 to 127, as said below
- panel_rare: bfloat16 [65536, 512], P(('site', 'col')), may hold values from -24 to 24
Outputs:
- grm_panel: float32 [512, 32768], P(None, ('site', 'col'))
Inputs may be any that keep to these rules, and one draw needn't show every extreme that they name: `block_tile`: the 16 listed blocks of device d in the site+col order (entries d * 16 to (d + 1) * 16 - 1) lie in distinct tiles; at most 2 of them lie in tiles t with one value of (t) mod 16.
All inputs are finite; a program needn't handle non-finite values.
Results may differ from a plain program's by a relative error of at most 0.0003.
Values may be sent and summed in bfloat16 or wider, within the bound.
No kernel may reach another device: no remote copies, remote signals or barrier semaphores. Data moves between devices by JAX's collectives and lax.ppermute only.
A program may use at most 192 MiB of HBM per device.

v0:
```python
import jax
import jax.numpy as jnp
from jax import lax
from jax.experimental import pallas as pl
from jax.experimental.pallas import tpu as pltpu
from jax.sharding import PartitionSpec as P


epsilon = 1e-05
BF = jnp.bfloat16
F32 = jnp.float32
NX = 4
NY = 4
NZ = 4
N_SITE = 8
N_COL = 16
TILE = 256
PANEL = 512
SBLK = 512
BLKS = 16
SLICE = TILE // N_SITE
VLIM = 60 * 1024 * 1024


def spec(shape, index_map):
    return pl.BlockSpec(shape, index_map)


def whole_vmem():
    return pl.BlockSpec(memory_space=pltpu.VMEM)


def pack_body(off_ref, x_ref, *rest):
    outs, turned = rest[:N_SITE], rest[N_SITE]
    for b in range(x_ref.shape[0]):
        turned[...] = x_ref[b].T
        for q in range(N_SITE):
            start = pl.multiple_of(off_ref[q], SLICE)
            outs[q][b * SLICE : (b + 1) * SLICE, :] = turned[pl.ds(start, SLICE), :]


def pack(rare_values, offsets):
    per = 2
    return pl.pallas_call(
        pack_body,
        grid_spec=pltpu.PrefetchScalarGridSpec(
            num_scalar_prefetch=1,
            grid=(BLKS // per,),
            in_specs=[spec((per, SBLK, TILE), lambda k, off: (k, 0, 0))],
            out_specs=[spec((per * SLICE, SBLK), lambda k, off: (k, 0))] * N_SITE,
            scratch_shapes=[pltpu.VMEM((TILE, SBLK), BF)],
        ),
        out_shape=[jax.ShapeDtypeStruct((BLKS * SLICE, SBLK), BF)] * N_SITE,
        compiler_params=pltpu.CompilerParams(vmem_limit_bytes=VLIM),
        cost_estimate=pl.CostEstimate(flops=0, bytes_accessed=8 << 20, transcendentals=0),
        name="pack_rare",
    )(offsets, rare_values)


def scale_body(x_ref, out_ref):
    rows, samples = x_ref.shape
    tiles = samples // TILE
    total = jnp.zeros((rows, TILE), F32)
    for t in range(tiles):
        total = total + x_ref[:, t * TILE : (t + 1) * TILE].astype(F32)
    freq = jnp.sum(total, axis=1, keepdims=True) / (2.0 * samples)
    scaling = lax.rsqrt(2.0 * freq * (1.0 - freq) + epsilon)
    mean = 2.0 * freq
    width = tiles // N_COL * TILE
    for t in range(tiles):
        scaled = ((x_ref[:, t * TILE : (t + 1) * TILE].astype(F32) - mean) * scaling).astype(BF)
        at = t // N_COL * TILE
        out_ref[t % N_COL, :, at : at + TILE] = scaled
        if t < PANEL // TILE:
            for c in range(N_COL):
                out_ref[c, :, width + t * TILE : width + (t + 1) * TILE] = scaled


def scale(common_geno):
    sites, samples = common_geno.shape
    rows = 16
    width = samples // N_COL + PANEL
    return pl.pallas_call(
        scale_body,
        grid=(sites // rows,),
        in_specs=[spec((rows, samples), lambda i: (i, 0))],
        out_specs=spec((N_COL, rows, width), lambda i: (0, i, 0)),
        out_shape=jax.ShapeDtypeStruct((N_COL, sites, width), BF),
        compiler_params=pltpu.CompilerParams(vmem_limit_bytes=VLIM),
        cost_estimate=pl.CostEstimate(flops=0, bytes_accessed=9 << 20, transcendentals=0),
        name="scale_common",
    )(common_geno)


def common_body(dest_ref, panel_ref, owned_ref, *rest):
    outs, turned = rest[:N_SITE], rest[N_SITE]
    step = pl.program_id(0)

    @pl.when(step == 0)
    def _():
        turned[...] = panel_ref[...].T

    part = jnp.dot(turned[...], owned_ref[...], preferred_element_type=F32)
    for q in range(N_SITE):

        @pl.when(step == q)
        def _():
            outs[q][...] = part


def common_product(received, dests):
    sites = received.shape[0] * received.shape[1]
    flat = received.reshape(sites, received.shape[2])
    last = (received.shape[2] - PANEL) // PANEL
    return pl.pallas_call(
        common_body,
        grid_spec=pltpu.PrefetchScalarGridSpec(
            num_scalar_prefetch=1,
            grid=(N_SITE,),
            in_specs=[
                spec((sites, PANEL), lambda q, dest: (0, last)),
                spec((sites, TILE), lambda q, dest: (0, dest[q])),
            ],
            out_specs=[spec((PANEL, TILE), lambda q, dest: (0, 0))] * N_SITE,
            scratch_shapes=[pltpu.VMEM((PANEL, sites), BF)],
        ),
        out_shape=[jax.ShapeDtypeStruct((PANEL, TILE), F32)] * N_SITE,
        compiler_params=pltpu.CompilerParams(vmem_limit_bytes=VLIM),
        cost_estimate=pl.CostEstimate(
            flops=2 * sites * PANEL * TILE * N_SITE, bytes_accessed=9 << 20, transcendentals=0
        ),
        name="common_product",
    )(dests, flat, flat)


HALF = 64


def rare_body(place_ref, *refs):
    slices = refs[:N_SITE]
    panels = refs[N_SITE : 2 * N_SITE]
    outs = refs[2 * N_SITE : 2 * N_SITE + 10]
    acc, made, sem = refs[2 * N_SITE + 10 :]
    acc[...] = jnp.zeros_like(acc)
    for q in range(N_SITE):
        made[...] = jnp.dot(
            slices[q][...], panels[q][:SBLK, :], preferred_element_type=F32
        )
        for k in range(BLKS):
            at = place_ref[q * BLKS + k]
            acc[at] = acc[at] + made[k * SLICE : (k + 1) * SLICE, :]
    copies = []
    for h in range(2):
        base = h * HALF
        up, down, keep1, keep3, own = outs[5 * h : 5 * h + 5]

        def unit(u, lo, hi):
            return acc.at[base + u * 16 + lo : base + u * 16 + hi]

        copies += [
            (unit(2, 0, 8), up.at[0:8]),
            (unit(1, 8, 16), up.at[8:16]),
            (unit(2, 8, 16), down.at[0:8]),
            (unit(3, 0, 8), down.at[8:16]),
            (unit(1, 0, 8), keep1),
            (unit(3, 8, 16), keep3),
            (unit(0, 0, 16), own),
        ]
    started = [
        pltpu.make_async_copy(src, dst, sem.at[i]) for i, (src, dst) in enumerate(copies)
    ]
    for one in started:
        one.start()
    for one in started:
        one.wait()


def rare_product(places, slices, panels):
    half = [16, 16, 8, 8, 16]
    return pl.pallas_call(
        rare_body,
        in_specs=[pl.BlockSpec(memory_space=pltpu.SMEM)] + [whole_vmem()] * (2 * N_SITE),
        out_specs=[pl.BlockSpec(memory_space=pl.ANY)] * 10,
        out_shape=[jax.ShapeDtypeStruct((n, SLICE, PANEL), F32) for n in half + half],
        scratch_shapes=[
            pltpu.VMEM((2 * HALF, SLICE, PANEL), F32),
            pltpu.VMEM((BLKS * SLICE, PANEL), F32),
            pltpu.SemaphoreType.DMA((14,)),
        ],
        compiler_params=pltpu.CompilerParams(vmem_limit_bytes=VLIM),
        cost_estimate=pl.CostEstimate(
            flops=2 * N_SITE * BLKS * SLICE * SBLK * PANEL, bytes_accessed=16 << 20, transcendentals=0
        ),
        name="rare_product",
    )(places, *slices, *panels)


def finish_body(turned_ref, *refs):
    parts, out_ref = refs[:N_SITE], refs[N_SITE]
    total = parts[0][...]
    for part in parts[1:]:
        total = total + part[...]
    out_ref[...] = (total + turned_ref[...].T) * (1.0 / 8192)


def finish(turned, parts):
    rows = PANEL // 2
    return pl.pallas_call(
        finish_body,
        grid=(2,),
        in_specs=[spec((TILE, rows), lambda i: (0, i))]
        + [spec((rows, TILE), lambda i: (i, 0))] * N_SITE,
        out_specs=spec((rows, TILE), lambda i: (i, 0)),
        out_shape=jax.ShapeDtypeStruct((PANEL, TILE), F32),
        compiler_params=pltpu.CompilerParams(vmem_limit_bytes=VLIM),
        cost_estimate=pl.CostEstimate(flops=0, bytes_accessed=6 << 20, transcendentals=0),
        name="finish",
    )(turned, *parts)


def along_site(dz, flip):
    return [
        (z * 2 + core, (z + dz) % NZ * 2 + (core ^ flip)) for z in range(NZ) for core in range(2)
    ]


def along_x(step):
    return [(x * NY + y, (x + step) % NX * NY + y) for x in range(NX) for y in range(NY)]


def along_y(step):
    return [(x * NY + y, x * NY + (y + step) % NY) for x in range(NX) for y in range(NY)]


def ring_open(up, down, perm):
    return lax.ppermute(up, "col", perm(1)), lax.ppermute(down, "col", perm(-1))


def ring_close(arrived, keep1, keep3, own, perm):
    from_low, from_high = arrived
    n = keep1.shape[0]
    low2 = lax.ppermute(keep1 + from_low[:n], "col", perm(1))
    high2 = lax.ppermute(keep3 + from_high[:n], "col", perm(-1))
    first = own[:n] + from_high[n:] + low2
    second = own[n:] + from_low[n:] + high2
    return first, second


def ring(up, down, keep1, keep3, own, perm):
    return ring_close(ring_open(up, down, perm), keep1, keep3, own, perm)


def second_ring(first, second, perm):
    own, one = first[:4], first[4:]
    two, three = second[:4], second[4:]
    up = jnp.concatenate([two[:2], one[2:]], axis=0)
    down = jnp.concatenate([two[2:], three[:2]], axis=0)
    return ring(up, down, one[:2], three[2:], own, perm)


def per_device(common_geno, rare_values, block_tile, panel_rare):
    site = lax.axis_index("site")
    col = lax.axis_index("col")
    z, core = site // 2, site % 2
    x, y = col // NY, col % NY
    order = [(dz, flip) for dz in range(NZ) for flip in range(2)]
    dests = jnp.stack([(z + dz) % NZ * 2 + (core ^ flip) for dz, flip in order]).astype(jnp.int32)

    tile_row = jnp.zeros((16, PANEL), BF).at[0, :BLKS].set(block_tile.astype(BF))
    panel_plus = jnp.concatenate([panel_rare, tile_row], axis=0)
    near = [panel_plus] + [
        lax.ppermute(panel_plus, "site", along_site(dz, 0)) for dz in range(1, NZ)
    ]

    scaled = scale(common_geno)
    scaled, offsets = lax.optimization_barrier((scaled, dests * SLICE))
    received = lax.all_to_all(scaled, "col", split_axis=0, concat_axis=0, tiled=True)

    packed = pack(rare_values, offsets)
    far = [lax.ppermute(one, "site", along_site(0, 1)) for one in near]
    panels = [(near, far)[flip][dz] for dz, flip in order]
    slices = [packed[0]] + [
        lax.ppermute(packed[q], "site", along_site(*order[q])) for q in range(1, N_SITE)
    ]

    tiles = jnp.stack([one[SBLK, :BLKS] for one in panels]).astype(jnp.int32).reshape(-1)
    tile_site, tile_col = tiles // N_COL, tiles % N_COL
    u = (tile_col // NY - x) % NX
    v = (tile_col % NY - y) % NY
    places = jnp.where(tile_site < 4, u * 16 + v * 4, HALF + v * 16 + u * 4) + tile_site % 4
    ring_parts = rare_product(places.astype(jnp.int32), slices, panels)

    ring_parts, dests = lax.optimization_barrier((ring_parts, dests))
    common = common_product(received, dests)
    open_a = ring_open(*ring_parts[:2], along_x)
    open_b = ring_open(*ring_parts[5:7], along_y)
    common = [common[0]] + [
        lax.ppermute(common[q], "site", along_site(*order[q])) for q in range(1, N_SITE)
    ]

    a = ring_close(open_a, *ring_parts[2:5], along_x)
    b = ring_close(open_b, *ring_parts[7:], along_y)
    a = second_ring(*a, along_y)
    b = second_ring(*b, along_x)
    reduced = jnp.concatenate([*a, *b], axis=0)
    turned = lax.all_to_all(reduced, "site", split_axis=0, concat_axis=0, tiled=True)
    return finish(turned.reshape(TILE, PANEL), common)


def solution(mesh):
    placed = (
        P(("site", "col"), None),
        P(("site", "col"), None, None),
        P(("site", "col")),
        P(("site", "col"), None),
    )
    return jax.shard_map(
        per_device, mesh=mesh, in_specs=placed, out_specs=P(None, ("site", "col")), check_vma=False
    )
```

profile of v0, /device:TPU:1, one launch (start us, length us, event | category | flops | bytes accessed | tf_op | source)
XLA Modules:
  0.0 258.9 jit_solution(6803951473601159991)
XLA Ops:
  0.7 1.1 fusion.1.refs_8_
  1.7 4.6 %collective-permute-start.5 = (bf16[528,512]{1,0:T(8,128)(2,1)S(1)}, bf16[528,512]{1,0:T(8,128)(2,1)S(1)}, u32[]{:S(2)}, u32[]{:S(2)}) collective-permute-start(bf16[528,512]{1,0:T(8,128)(2,1)S(1)} %fusion.1.refs_8_), channel_id=1, source_target_pairs={{0,96},{16,112},{32,0},{48,16},{64,32},{80,48},{96,64},{112,80},{1... | collective-permute-start | bytes 1622024 | tf_op jit(solution)/shard_map/ppermute | solution.py:272
  6.4 0.7 collective-permute-start.1
  7.8 5.8 %scale_common.1 = bf16[16,64,2560]{2,1,0:T(8,128)(2,1)} custom-call(bf16[64,32768]{1,0:T(8,128)(2,1)} %x_ref.2), custom_call_target="tpu_custom_call" | custom-call | bytes 9437184 | tf_op jit(solution)/shard_map/scale_common/pallas_call | solution.py:83
  13.6 7.8 %pack_rare.1 = (bf16[512,512]{1,0:T(8,128)(2,1)}, bf16[512,512]{1,0:T(8,128)(2,1)}, bf16[512,512]{1,0:T(8,128)(2,1)}, bf16[512,512]{1,0:T(8,128)(2,1)}, bf16[512...) custom-call(s32[8]{0:T(128)} %broadcast_multiply_fusion.off_ref, ...), custom_call_target="tpu_custom_call" | custom-call | bytes 8388608 | tf_op jit(solution)/shard_map/pack_rare/pallas_call | solution.py:44
  21.4 1.6 collective-permute-start.7
  23.1 5.7 %collective-permute-done.5.refs_14_ = bf16[528,512]{1,0:T(8,128)(2,1)S(1)} collective-permute-done((bf16[528,512]{1,0:T(8,128)(2,1)S(1)}, bf16[528,512]{1,0:T(8,128)(2,1)S(1)}, u32[]{:S(2)}, u32[]{:S(2)}) %collective-permute-start.5) | collective-permute-done | bytes 540704 | tf_op jit(solution)/shard_map/ppermute | solution.py:272
  28.8 1.7 collective-permute-start.6
  30.6 2.5 collective-permute-done.1.refs_10_
  33.1 0.8 collective-permute-start.2
  33.9 6.8 %all-to-all-start.1 = ((bf16[16,64,2560]{2,1,0:T(8,128)(2,1)}), bf16[16,64,2560]{2,1,0:T(8,128)(2,1)}, u32[]{:S(2)}, u32[]{:S(2)}) async-start(bf16[16,64,2560]{2,1,0:T(8,128)(2,1)} %scale_common.1), calls=%async_computation.1 | async-start | bytes 10485760 | tf_op jit(solution)/shard_map/all_to_all | solution.py:277
  40.7 8.1 %collective-permute-done.8.refs_2_ = bf16[512,512]{1,0:T(8,128)(2,1)} collective-permute-done((bf16[512,512]{1,0:T(8,128)(2,1)}, bf16[512,512]{1,0:T(8,128)(2,1)}, u32[]{:S(2)}, u32[]{:S(2)}) %collective-permute-start.8) | collective-permute-done | bytes 524320 | tf_op jit(solution)/shard_map/ppermute | solution.py:283
  48.8 1.4 collective-permute-start.10
  50.2 2.7 %collective-permute-start.11 = (bf16[512,512]{1,0:T(8,128)(2,1)}, bf16[512,512]{1,0:T(8,128)(2,1)}, u32[]{:S(2)}, u32[]{:S(2)}) collective-permute-start(bf16[512,512]{1,0:T(8,128)(2,1)} %get-tuple-element.62), channel_id=1, source_target_pairs={{0,80},{16,64},{32,112},{48,96},{64,16},{80,0},{96,48},{112,32},{1... | collective-permute-start | bytes 1572872 | tf_op jit(solution)/shard_map/ppermute | solution.py:283
  53.0 2.1 collective-permute-start.12
  55.7 0.7 slice.210
  56.4 0.7 slice.208
  57.8 29.3 %collective-permute-done.9.refs_3_ = bf16[512,512]{1,0:T(8,128)(2,1)} collective-permute-done((bf16[512,512]{1,0:T(8,128)(2,1)}, bf16[512,512]{1,0:T(8,128)(2,1)}, u32[]{:S(2)}, u32[]{:S(2)}) %collective-permute-start.9) | collective-permute-done | bytes 524320 | tf_op jit(solution)/shard_map/ppermute | solution.py:283
  87.1 1.1 collective-permute-done.12.refs_6_
  88.2 11.3 %collective-permute-done.13.refs_7_ = bf16[512,512]{1,0:T(8,128)(2,1)} collective-permute-done((bf16[512,512]{1,0:T(8,128)(2,1)}, bf16[512,512]{1,0:T(8,128)(2,1)}, u32[]{:S(2)}, u32[]{:S(2)}) %collective-permute-start.13) | collective-permute-done | bytes 524320 | tf_op jit(solution)/shard_map/ppermute | solution.py:283
  99.5 9.6 %rare_product.1 = (f32[16,32,512]{2,1,0:T(8,128)}, f32[16,32,512]{2,1,0:T(8,128)}, f32[8,32,512]{2,1,0:T(8,128)}, f32[8,32,512]{2,1,0:T(8,128)}, f32[16,32,512]{...) custom-call(s32[128]{0:T(128)} %fusion.10.place_ref, ...), custom_call_target="tpu_custom_call" | custom-call | flops 2147483648 | bytes 16777216 | tf_op jit(solution)/shard_map/rare_product/pallas_call | solution.py:180
  109.1 2.6 collective-permute-start.14
  111.6 2.7 %collective-permute-start.22 = (f32[16,32,512]{2,1,0:T(8,128)}, f32[16,32,512]{2,1,0:T(8,128)S(1)}, u32[]{:S(2)}, u32[]{:S(2)}) collective-permute-start(f32[16,32,512]{2,1,0:T(8,128)} %get-tuple-element.81), channel_id=1, source_target_pairs={{0,3},{1,0},{2,1},{3,2},{4,7},{5,4},{6,5},{7,6},{8,11},{9,8},{10,9... | collective-permute-start | bytes 3145736 | tf_op jit(solution)/shard_map/ppermute | solution.py:236
  114.4 19.7 %collective-permute-done.14 = f32[16,32,512]{2,1,0:T(8,128)S(1)} collective-permute-done((f32[16,32,512]{2,1,0:T(8,128)}, f32[16,32,512]{2,1,0:T(8,128)S(1)}, u32[]{:S(2)}, u32[]{:S(2)}) %collective-permute-start.14) | collective-permute-done | bytes 1048608 | tf_op jit(solution)/shard_map/ppermute | solution.py:236
  134.1 1.1 slice_add_fusion.4
  135.2 11.2 %collective-permute-start.17 = (f32[8,32,512]{2,1,0:T(8,128)S(1)}, f32[8,32,512]{2,1,0:T(8,128)S(1)}, u32[]{:S(2)}, u32[]{:S(2)}) collective-permute-start(f32[8,32,512]{2,1,0:T(8,128)S(1)} %slice_add_fusion.4), channel_id=1, source_target_pairs={{0,12},{1,13},{2,14},{3,15},{4,0},{5,1},{6,2},{7,3},{8,4},{9,5},{1... | collective-permute-start | bytes 1572872 | tf_op jit(solution)/shard_map/ppermute | solution.py:243
  146.8 0.7 copy-done.11
  147.7 1.0 collective-permute-start.24
  148.6 7.9 %collective-permute-done.17 = f32[8,32,512]{2,1,0:T(8,128)S(1)} collective-permute-done((f32[8,32,512]{2,1,0:T(8,128)S(1)}, f32[8,32,512]{2,1,0:T(8,128)S(1)}, u32[]{:S(2)}, u32[]{:S(2)}) %collective-permute-start.17) | collective-permute-done | bytes 524320 | tf_op jit(solution)/shard_map/ppermute | solution.py:243
  156.5 3.3 %collective-permute-done.16 = f32[8,32,512]{2,1,0:T(8,128)S(1)} collective-permute-done((f32[8,32,512]{2,1,0:T(8,128)S(1)}, f32[8,32,512]{2,1,0:T(8,128)S(1)}, u32[]{:S(2)}, u32[]{:S(2)}) %collective-permute-start.16) | collective-permute-done | bytes 524320 | tf_op jit(solution)/shard_map/ppermute | solution.py:242
  160.3 0.8 collective-permute-done.24
  161.5 2.1 collective-permute-start.26
  163.6 1.9 collective-permute-done.18
  165.5 1.8 collective-permute-start.21
  167.5 2.6 collective-permute-start.29
  170.2 3.7 %collective-permute-done.19 = f32[4,32,512]{2,1,0:T(8,128)S(1)} collective-permute-done((f32[4,32,512]{2,1,0:T(8,128)S(1)}, f32[4,32,512]{2,1,0:T(8,128)S(1)}, u32[]{:S(2)}, u32[]{:S(2)}) %collective-permute-start.19) | collective-permute-done | bytes 262176 | tf_op jit(solution)/shard_map/ppermute | solution.py:236
  174.0 10.3 %common_product.1 = (f32[512,256]{1,0:T(8,128)}, f32[512,256]{1,0:T(8,128)}, f32[512,256]{1,0:T(8,128)}, f32[512,256]{1,0:T(8,128)}, f32[512,256]{1,0:T(8,128)},...) custom-call(s32[8]{0:T(128)} %copy-done.19, bf16[1024,2560]{1,0:T(8,128)(2,1)} %bitcast.10.panel_ref.owned_ref, ...), custom_call_target="tpu_custom_call" | custom-call | flops 2147483648 | bytes 9437184 | tf_op jit(solution)/shard_map/common_product/pallas_call | solution.py:115
  184.4 4.6 %collective-permute-start.30 = (f32[512,256]{1,0:T(8,128)}, f32[512,256]{1,0:T(8,128)S(1)}, u32[]{:S(2)}, u32[]{:S(2)}) collective-permute-start(f32[512,256]{1,0:T(8,128)} %get-tuple-element.88), channel_id=1, source_target_pairs={{0,16},{16,0},{32,48},{48,32},{64,80},{80,64},{96,112},{112,96},{1... | collective-permute-start | bytes 1572872 | tf_op jit(solution)/shard_map/ppermute | solution.py:298
  189.0 3.9 %collective-permute-start.31 = (f32[512,256]{1,0:T(8,128)}, f32[512,256]{1,0:T(8,128)S(1)}, u32[]{:S(2)}, u32[]{:S(2)}) collective-permute-start(f32[512,256]{1,0:T(8,128)} %get-tuple-element.89), channel_id=1, source_target_pairs={{0,32},{16,48},{32,64},{48,80},{64,96},{80,112},{96,0},{112,16},{1... | collective-permute-start | bytes 1572872 | tf_op jit(solution)/shard_map/ppermute | solution.py:298
  193.1 5.8 %collective-permute-done.28 = f32[2,32,512]{2,1,0:T(8,128)S(1)} collective-permute-done((f32[2,32,512]{2,1,0:T(8,128)S(1)}, f32[2,32,512]{2,1,0:T(8,128)S(1)}, u32[]{:S(2)}, u32[]{:S(2)}) %collective-permute-start.28) | collective-permute-done | bytes 131104 | tf_op jit(solution)/shard_map/ppermute | solution.py:242
  199.0 2.5 collective-permute-start.32
  201.5 2.6 collective-permute-start.33
  204.2 2.0 collective-permute-start.35
  206.3 1.8 collective-permute-done.31.refs_2_
  208.0 2.5 collective-permute-start.36
  210.6 43.6 %all_to_all.10 = f32[8,32,512]{2,1,0:T(8,128)} all-to-all(f32[8,32,512]{2,1,0:T(8,128)S(1)} %pad_maximum_fusion), channel_id=1, replica_groups=mesh['site'=8,'col'=16] {'site'}, dimensions={0} | all-to-all | bytes 1048576 | tf_op jit(solution)/shard_map/all_to_all | solution.py:306
  254.3 0.7 copy-done.13
  255.7 3.2 %finish.1 = f32[512,256]{1,0:T(8,128)} custom-call(f32[256,512]{1,0:T(8,128)} %bitcast.12, f32[512,256]{1,0:T(8,128)} %get-tuple-element.87.refs_0_, f32[512,256]{1,0:T(8,128)} %copy-done.9, f32[512,256]{1,0:T(8,128)} %copy-done.10, f32[512,256]{1,0:T(8,128)} %copy-done.13, f32[512,256]{1,0:T(8,128)} %copy-done.15, f32[512,256]{1,0:T(8,128)} %copy-done.16, ...), custom_call_target="tpu_custom_call" | custom-call | bytes 6291456 | tf_op jit(solution)/shard_map/finish/pallas_call | solution.py:208
  (114 shorter events, 5.7 us)
Async XLA Ops:
  1.7 21.3 %copy-start = (bf16[528,512]{1,0:T(8,128)(2,1)}, bf16[528,512]{1,0:T(8,128)(2,1)S(1)}, u32[]{:S(2)}) copy-start(bf16[528,512]{1,0:T(8,128)(2,1)S(1)} %fusion.1.refs_8_) | copy-start | bytes 1622020
  1.7 27.0 %collective-permute-start.5 = (bf16[528,512]{1,0:T(8,128)(2,1)S(1)}, bf16[528,512]{1,0:T(8,128)(2,1)S(1)}, u32[]{:S(2)}, u32[]{:S(2)}) collective-permute-start(bf16[528,512]{1,0:T(8,128)(2,1)S(1)} %fusion.1.refs_8_), channel_id=1, source_target_pairs={{0,96},{16,112},{32,0},{48,16},{64,32},{80,48},{96,64},{112,80},{1... | collective-permute-start | bytes 1622024 | tf_op jit(solution)/shard_map/ppermute | solution.py:272
  6.4 24.1 %collective-permute-start.3 = (bf16[528,512]{1,0:T(8,128)(2,1)S(1)}, bf16[528,512]{1,0:T(8,128)(2,1)S(1)}, u32[]{:S(2)}, u32[]{:S(2)}) collective-permute-start(bf16[528,512]{1,0:T(8,128)(2,1)S(1)} %fusion.1.refs_8_), channel_id=1, source_target_pairs={{0,64},{16,80},{32,96},{48,112},{64,0},{80,16},{96,32},{112,48},{1... | collective-permute-start | bytes 1622024 | tf_op jit(solution)/shard_map/ppermute | solution.py:272
  6.4 26.7 %collective-permute-start.1 = (bf16[528,512]{1,0:T(8,128)(2,1)S(1)}, bf16[528,512]{1,0:T(8,128)(2,1)S(1)}, u32[]{:S(2)}, u32[]{:S(2)}) collective-permute-start(bf16[528,512]{1,0:T(8,128)(2,1)S(1)} %fusion.1.refs_8_), channel_id=1, source_target_pairs={{0,32},{16,48},{32,64},{48,80},{64,96},{80,112},{96,0},{112,16},{1... | collective-permute-start | bytes 1622024 | tf_op jit(solution)/shard_map/ppermute | solution.py:272
  21.4 12.5 %collective-permute-start.7 = (bf16[512,512]{1,0:T(8,128)(2,1)}, bf16[512,512]{1,0:T(8,128)(2,1)}, u32[]{:S(2)}, u32[]{:S(2)}) collective-permute-start(bf16[512,512]{1,0:T(8,128)(2,1)} %get-tuple-element.58), channel_id=1, source_target_pairs={{0,16},{16,0},{32,48},{48,32},{64,80},{80,64},{96,112},{112,96},{1... | collective-permute-start | bytes 1572872 | tf_op jit(solution)/shard_map/ppermute | solution.py:283
  23.0 25.8 %collective-permute-start = (bf16[528,512]{1,0:T(8,128)(2,1)S(1)}, bf16[528,512]{1,0:T(8,128)(2,1)S(1)}, u32[]{:S(2)}, u32[]{:S(2)}) collective-permute-start(bf16[528,512]{1,0:T(8,128)(2,1)S(1)} %fusion.1.refs_8_), channel_id=1, source_target_pairs={{0,16},{16,0},{32,48},{48,32},{64,80},{80,64},{96,112},{112,96},{1... | collective-permute-start | bytes 1622024 | tf_op jit(solution)/shard_map/ppermute | solution.py:280
  28.8 26.9 %copy-start.3 = (bf16[528,512]{1,0:T(8,128)(2,1)}, bf16[528,512]{1,0:T(8,128)(2,1)S(1)}, u32[]{:S(2)}) copy-start(bf16[528,512]{1,0:T(8,128)(2,1)S(1)} %collective-permute-done.5.refs_14_) | copy-start | bytes 1622020
  28.8 21.4 %collective-permute-start.6 = (bf16[528,512]{1,0:T(8,128)(2,1)S(1)}, bf16[528,512]{1,0:T(8,128)(2,1)S(1)}, u32[]{:S(2)}, u32[]{:S(2)}) collective-permute-start(bf16[528,512]{1,0:T(8,128)(2,1)S(1)} %collective-permute-done.5.refs_14_), channel_id=1, source_target_pairs={{0,16},{16,0},{32,48},{48,32},{64,80},{80,64},{96,112},{112,96},{1... | collective-permute-start | bytes 1622024 | tf_op jit(solution)/shard_map/ppermute | solution.py:280
  30.5 25.2 %copy-start.4 = (bf16[528,512]{1,0:T(8,128)(2,1)}, bf16[528,512]{1,0:T(8,128)(2,1)S(1)}, u32[]{:S(2)}) copy-start(bf16[528,512]{1,0:T(8,128)(2,1)S(1)} %collective-permute-done.3.refs_12_) | copy-start | bytes 1622020
  30.5 22.5 %collective-permute-start.4 = (bf16[528,512]{1,0:T(8,128)(2,1)S(1)}, bf16[528,512]{1,0:T(8,128)(2,1)}, u32[]{:S(2)}, u32[]{:S(2)}) collective-permute-start(bf16[528,512]{1,0:T(8,128)(2,1)S(1)} %collective-permute-done.3.refs_12_), channel_id=1, source_target_pairs={{0,16},{16,0},{32,48},{48,32},{64,80},{80,64},{96,112},{112,96},{1... | collective-permute-start | bytes 1622024 | tf_op jit(solution)/shard_map/ppermute | solution.py:280
  33.1 22.6 %copy-start.5 = (bf16[528,512]{1,0:T(8,128)(2,1)}, bf16[528,512]{1,0:T(8,128)(2,1)S(1)}, u32[]{:S(2)}) copy-start(bf16[528,512]{1,0:T(8,128)(2,1)S(1)} %collective-permute-done.1.refs_10_) | copy-start | bytes 1622020
  33.1 21.9 %collective-permute-start.2 = (bf16[528,512]{1,0:T(8,128)(2,1)S(1)}, bf16[528,512]{1,0:T(8,128)(2,1)}, u32[]{:S(2)}, u32[]{:S(2)}) collective-permute-start(bf16[528,512]{1,0:T(8,128)(2,1)S(1)} %collective-permute-done.1.refs_10_), channel_id=1, source_target_pairs={{0,16},{16,0},{32,48},{48,32},{64,80},{80,64},{96,112},{112,96},{1... | collective-permute-start | bytes 1622024 | tf_op jit(solution)/shard_map/ppermute | solution.py:280
  33.9 14.9 %collective-permute-start.8 = (bf16[512,512]{1,0:T(8,128)(2,1)}, bf16[512,512]{1,0:T(8,128)(2,1)}, u32[]{:S(2)}, u32[]{:S(2)}) collective-permute-start(bf16[512,512]{1,0:T(8,128)(2,1)} %get-tuple-element.59), channel_id=1, source_target_pairs={{0,32},{16,48},{32,64},{48,80},{64,96},{80,112},{96,0},{112,16},{1... | collective-permute-start | bytes 1572872 | tf_op jit(solution)/shard_map/ppermute | solution.py:283
  33.9 140.1 %all-to-all-start.1 = ((bf16[16,64,2560]{2,1,0:T(8,128)(2,1)}), bf16[16,64,2560]{2,1,0:T(8,128)(2,1)}, u32[]{:S(2)}, u32[]{:S(2)}) async-start(bf16[16,64,2560]{2,1,0:T(8,128)(2,1)} %scale_common.1), calls=%async_computation.1 | async-start | bytes 10485760 | tf_op jit(solution)/shard_map/all_to_all | solution.py:277
  48.8 38.3 %collective-permute-start.9 = (bf16[512,512]{1,0:T(8,128)(2,1)}, bf16[512,512]{1,0:T(8,128)(2,1)}, u32[]{:S(2)}, u32[]{:S(2)}) collective-permute-start(bf16[512,512]{1,0:T(8,128)(2,1)} %get-tuple-element.60), channel_id=1, source_target_pairs={{0,48},{16,32},{32,80},{48,64},{64,112},{80,96},{96,16},{112,0},{1... | collective-permute-start | bytes 1572872 | tf_op jit(solution)/shard_map/ppermute | solution.py:283
  48.8 50.6 %copy-start.6 = (bf16[528,512]{1,0:T(8,128)(2,1)}, bf16[528,512]{1,0:T(8,128)(2,1)S(1)}, u32[]{:S(2)}) copy-start(bf16[528,512]{1,0:T(8,128)(2,1)S(1)} %collective-permute-done.refs_9_) | copy-start | bytes 1622020
  48.8 38.3 %collective-permute-start.10 = (bf16[512,512]{1,0:T(8,128)(2,1)}, bf16[512,512]{1,0:T(8,128)(2,1)S(1)}, u32[]{:S(2)}, u32[]{:S(2)}) collective-permute-start(bf16[512,512]{1,0:T(8,128)(2,1)} %get-tuple-element.61), channel_id=1, source_target_pairs={{0,64},{16,80},{32,96},{48,112},{64,0},{80,16},{96,32},{112,48},{1... | collective-permute-start | bytes 1572872 | tf_op jit(solution)/shard_map/ppermute | solution.py:283
  50.2 49.2 %copy-start.7 = (bf16[528,512]{1,0:T(8,128)(2,1)}, bf16[528,512]{1,0:T(8,128)(2,1)S(1)}, u32[]{:S(2)}) copy-start(bf16[528,512]{1,0:T(8,128)(2,1)S(1)} %collective-permute-done.6.refs_15_) | copy-start | bytes 1622020
  50.2 36.9 %collective-permute-start.11 = (bf16[512,512]{1,0:T(8,128)(2,1)}, bf16[512,512]{1,0:T(8,128)(2,1)}, u32[]{:S(2)}, u32[]{:S(2)}) collective-permute-start(bf16[512,512]{1,0:T(8,128)(2,1)} %get-tuple-element.62), channel_id=1, source_target_pairs={{0,80},{16,64},{32,112},{48,96},{64,16},{80,0},{96,48},{112,32},{1... | collective-permute-start | bytes 1572872 | tf_op jit(solution)/shard_map/ppermute | solution.py:283
  53.0 35.2 %collective-permute-start.12 = (bf16[512,512]{1,0:T(8,128)(2,1)}, bf16[512,512]{1,0:T(8,128)(2,1)}, u32[]{:S(2)}, u32[]{:S(2)}) collective-permute-start(bf16[512,512]{1,0:T(8,128)(2,1)} %get-tuple-element.63), channel_id=1, source_target_pairs={{0,96},{16,112},{32,0},{48,16},{64,32},{80,48},{96,64},{112,80},{1... | collective-permute-start | bytes 1572872 | tf_op jit(solution)/shard_map/ppermute | solution.py:283
  55.0 44.4 %collective-permute-start.13 = (bf16[512,512]{1,0:T(8,128)(2,1)}, bf16[512,512]{1,0:T(8,128)(2,1)}, u32[]{:S(2)}, u32[]{:S(2)}) collective-permute-start(bf16[512,512]{1,0:T(8,128)(2,1)} %get-tuple-element.64), channel_id=1, source_target_pairs={{0,112},{16,96},{32,16},{48,0},{64,48},{80,32},{96,80},{112,64},{1... | collective-permute-start | bytes 1572872 | tf_op jit(solution)/shard_map/ppermute | solution.py:283
  109.1 37.4 %copy-start.14 = (f32[8,32,512]{2,1,0:T(8,128)S(1)}, f32[8,32,512]{2,1,0:T(8,128)}, u32[]{:S(2)}) copy-start(f32[8,32,512]{2,1,0:T(8,128)} %get-tuple-element.77) | copy-start | bytes 1572868
  109.1 25.0 %collective-permute-start.14 = (f32[16,32,512]{2,1,0:T(8,128)}, f32[16,32,512]{2,1,0:T(8,128)S(1)}, u32[]{:S(2)}, u32[]{:S(2)}) collective-permute-start(f32[16,32,512]{2,1,0:T(8,128)} %get-tuple-element.76), channel_id=1, source_target_pairs={{0,12},{1,13},{2,14},{3,15},{4,0},{5,1},{6,2},{7,3},{8,4},{9,5},{1... | collective-permute-start | bytes 3145736 | tf_op jit(solution)/shard_map/ppermute | solution.py:236
  111.6 34.8 %collective-permute-start.15 = (f32[16,32,512]{2,1,0:T(8,128)}, f32[16,32,512]{2,1,0:T(8,128)S(1)}, u32[]{:S(2)}, u32[]{:S(2)}) collective-permute-start(f32[16,32,512]{2,1,0:T(8,128)} %get-tuple-element.78), channel_id=1, source_target_pairs={{0,4},{1,5},{2,6},{3,7},{4,8},{5,9},{6,10},{7,11},{8,12},{9,13},{1... | collective-permute-start | bytes 3145736 | tf_op jit(solution)/shard_map/ppermute | solution.py:236
  111.6 35.0 %collective-permute-start.22 = (f32[16,32,512]{2,1,0:T(8,128)}, f32[16,32,512]{2,1,0:T(8,128)S(1)}, u32[]{:S(2)}, u32[]{:S(2)}) collective-permute-start(f32[16,32,512]{2,1,0:T(8,128)} %get-tuple-element.81), channel_id=1, source_target_pairs={{0,3},{1,0},{2,1},{3,2},{4,7},{5,4},{6,5},{7,6},{8,11},{9,8},{10,9... | collective-permute-start | bytes 3145736 | tf_op jit(solution)/shard_map/ppermute | solution.py:236
  114.4 32.5 %collective-permute-start.23 = (f32[16,32,512]{2,1,0:T(8,128)}, f32[16,32,512]{2,1,0:T(8,128)S(1)}, u32[]{:S(2)}, u32[]{:S(2)}) collective-permute-start(f32[16,32,512]{2,1,0:T(8,128)} %get-tuple-element.83), channel_id=1, source_target_pairs={{0,1},{1,2},{2,3},{3,0},{4,5},{5,6},{6,7},{7,4},{8,9},{9,10},{10,1... | collective-permute-start | bytes 3145736 | tf_op jit(solution)/shard_map/ppermute | solution.py:236
  135.2 21.2 %collective-permute-start.17 = (f32[8,32,512]{2,1,0:T(8,128)S(1)}, f32[8,32,512]{2,1,0:T(8,128)S(1)}, u32[]{:S(2)}, u32[]{:S(2)}) collective-permute-start(f32[8,32,512]{2,1,0:T(8,128)S(1)} %slice_add_fusion.4), channel_id=1, source_target_pairs={{0,12},{1,13},{2,14},{3,15},{4,0},{5,1},{6,2},{7,3},{8,4},{9,5},{1... | collective-permute-start | bytes 1572872 | tf_op jit(solution)/shard_map/ppermute | solution.py:243
  146.5 13.2 %collective-permute-start.16 = (f32[8,32,512]{2,1,0:T(8,128)S(1)}, f32[8,32,512]{2,1,0:T(8,128)S(1)}, u32[]{:S(2)}, u32[]{:S(2)}) collective-permute-start(f32[8,32,512]{2,1,0:T(8,128)S(1)} %slice_add_fusion.6), channel_id=1, source_target_pairs={{0,4},{1,5},{2,6},{3,7},{4,8},{5,9},{6,10},{7,11},{8,12},{9,13},{1... | collective-permute-start | bytes 1572872 | tf_op jit(solution)/shard_map/ppermute | solution.py:242
  146.8 13.5 %collective-permute-start.25 = (f32[8,32,512]{2,1,0:T(8,128)S(1)}, f32[8,32,512]{2,1,0:T(8,128)S(1)}, u32[]{:S(2)}, u32[]{:S(2)}) collective-permute-start(f32[8,32,512]{2,1,0:T(8,128)S(1)} %slice_add_fusion), channel_id=1, source_target_pairs={{0,3},{1,0},{2,1},{3,2},{4,7},{5,4},{6,5},{7,6},{8,11},{9,8},{10,9... | collective-permute-start | bytes 1572872 | tf_op jit(solution)/shard_map/ppermute | solution.py:243
  147.7 13.4 %collective-permute-start.24 = (f32[8,32,512]{2,1,0:T(8,128)S(1)}, f32[8,32,512]{2,1,0:T(8,128)S(1)}, u32[]{:S(2)}, u32[]{:S(2)}) collective-permute-start(f32[8,32,512]{2,1,0:T(8,128)S(1)} %slice_add_fusion.2), channel_id=1, source_target_pairs={{0,1},{1,2},{2,3},{3,0},{4,5},{5,6},{6,7},{7,4},{8,9},{9,10},{10,1... | collective-permute-start | bytes 1572872 | tf_op jit(solution)/shard_map/ppermute | solution.py:242
  160.2 5.3 %collective-permute-start.18 = (f32[4,32,512]{2,1,0:T(8,128)S(1)}, f32[4,32,512]{2,1,0:T(8,128)S(1)}, u32[]{:S(2)}, u32[]{:S(2)}) collective-permute-start(f32[4,32,512]{2,1,0:T(8,128)S(1)} %concatenate.26), channel_id=1, source_target_pairs={{0,3},{1,0},{2,1},{3,2},{4,7},{5,4},{6,5},{7,6},{8,11},{9,8},{10,9... | collective-permute-start | bytes 786440 | tf_op jit(solution)/shard_map/ppermute | solution.py:236
  161.5 6.0 %collective-permute-start.26 = (f32[4,32,512]{2,1,0:T(8,128)S(1)}, f32[4,32,512]{2,1,0:T(8,128)S(1)}, u32[]{:S(2)}, u32[]{:S(2)}) collective-permute-start(f32[4,32,512]{2,1,0:T(8,128)S(1)} %concatenate.27), channel_id=1, source_target_pairs={{0,12},{1,13},{2,14},{3,15},{4,0},{5,1},{6,2},{7,3},{8,4},{9,5},{1... | collective-permute-start | bytes 786440 | tf_op jit(solution)/shard_map/ppermute | solution.py:236
  165.5 4.7 %collective-permute-start.21 = (f32[2,32,512]{2,1,0:T(8,128)S(1)}, f32[2,32,512]{2,1,0:T(8,128)S(1)}, u32[]{:S(2)}, u32[]{:S(2)}) collective-permute-start(f32[2,32,512]{2,1,0:T(8,128)S(1)} %get-tuple-element.104), channel_id=1, source_target_pairs={{0,3},{1,0},{2,1},{3,2},{4,7},{5,4},{6,5},{7,6},{8,11},{9,8},{10,9... | collective-permute-start | bytes 393224 | tf_op jit(solution)/shard_map/ppermute | solution.py:243
  167.4 6.5 %collective-permute-start.19 = (f32[4,32,512]{2,1,0:T(8,128)S(1)}, f32[4,32,512]{2,1,0:T(8,128)S(1)}, u32[]{:S(2)}, u32[]{:S(2)}) collective-permute-start(f32[4,32,512]{2,1,0:T(8,128)S(1)} %pad_maximum_fusion.1), channel_id=1, source_target_pairs={{0,1},{1,2},{2,3},{3,0},{4,5},{5,6},{6,7},{7,4},{8,9},{9,10},{10,1... | collective-permute-start | bytes 786440 | tf_op jit(solution)/shard_map/ppermute | solution.py:236
  167.5 25.4 %collective-permute-start.29 = (f32[2,32,512]{2,1,0:T(8,128)S(1)}, f32[2,32,512]{2,1,0:T(8,128)S(1)}, u32[]{:S(2)}, u32[]{:S(2)}) collective-permute-start(f32[2,32,512]{2,1,0:T(8,128)S(1)} %get-tuple-element.106), channel_id=1, source_target_pairs={{0,12},{1,13},{2,14},{3,15},{4,0},{5,1},{6,2},{7,3},{8,4},{9,5},{1... | collective-permute-start | bytes 393224 | tf_op jit(solution)/shard_map/ppermute | solution.py:243
  170.1 22.8 %collective-permute-start.27 = (f32[4,32,512]{2,1,0:T(8,128)S(1)}, f32[4,32,512]{2,1,0:T(8,128)S(1)}, u32[]{:S(2)}, u32[]{:S(2)}) collective-permute-start(f32[4,32,512]{2,1,0:T(8,128)S(1)} %pad_maximum_fusion.2), channel_id=1, source_target_pairs={{0,4},{1,5},{2,6},{3,7},{4,8},{5,9},{6,10},{7,11},{8,12},{9,13},{1... | collective-permute-start | bytes 786440 | tf_op jit(solution)/shard_map/ppermute | solution.py:236
  174.0 19.1 %collective-permute-start.20 = (f32[2,32,512]{2,1,0:T(8,128)S(1)}, f32[2,32,512]{2,1,0:T(8,128)S(1)}, u32[]{:S(2)}, u32[]{:S(2)}) collective-permute-start(f32[2,32,512]{2,1,0:T(8,128)S(1)} %get-tuple-element.99), channel_id=1, source_target_pairs={{0,1},{1,2},{2,3},{3,0},{4,5},{5,6},{6,7},{7,4},{8,9},{9,10},{10,1... | collective-permute-start | bytes 393224 | tf_op jit(solution)/shard_map/ppermute | solution.py:242
  184.4 23.7 %copy-start.20 = (f32[512,256]{1,0:T(8,128)S(1)}, f32[512,256]{1,0:T(8,128)}, u32[]{:S(2)}) copy-start(f32[512,256]{1,0:T(8,128)} %get-tuple-element.94) | copy-start | bytes 1572868
  184.4 19.9 %collective-permute-start.30 = (f32[512,256]{1,0:T(8,128)}, f32[512,256]{1,0:T(8,128)S(1)}, u32[]{:S(2)}, u32[]{:S(2)}) collective-permute-start(f32[512,256]{1,0:T(8,128)} %get-tuple-element.88), channel_id=1, source_target_pairs={{0,16},{16,0},{32,48},{48,32},{64,80},{80,64},{96,112},{112,96},{1... | collective-permute-start | bytes 1572872 | tf_op jit(solution)/shard_map/ppermute | solution.py:298
  189.0 19.1 %collective-permute-start.31 = (f32[512,256]{1,0:T(8,128)}, f32[512,256]{1,0:T(8,128)S(1)}, u32[]{:S(2)}, u32[]{:S(2)}) collective-permute-start(f32[512,256]{1,0:T(8,128)} %get-tuple-element.89), channel_id=1, source_target_pairs={{0,32},{16,48},{32,64},{48,80},{64,96},{80,112},{96,0},{112,16},{1... | collective-permute-start | bytes 1572872 | tf_op jit(solution)/shard_map/ppermute | solution.py:298
  193.0 6.0 %collective-permute-start.28 = (f32[2,32,512]{2,1,0:T(8,128)S(1)}, f32[2,32,512]{2,1,0:T(8,128)S(1)}, u32[]{:S(2)}, u32[]{:S(2)}) collective-permute-start(f32[2,32,512]{2,1,0:T(8,128)S(1)} %get-tuple-element.101), channel_id=1, source_target_pairs={{0,4},{1,5},{2,6},{3,7},{4,8},{5,9},{6,10},{7,11},{8,12},{9,13},{1... | collective-permute-start | bytes 393224 | tf_op jit(solution)/shard_map/ppermute | solution.py:242
  199.0 55.2 %collective-permute-start.32 = (f32[512,256]{1,0:T(8,128)}, f32[512,256]{1,0:T(8,128)S(1)}, u32[]{:S(2)}, u32[]{:S(2)}) collective-permute-start(f32[512,256]{1,0:T(8,128)} %get-tuple-element.90), channel_id=1, source_target_pairs={{0,48},{16,32},{32,80},{48,64},{64,112},{80,96},{96,16},{112,0},{1... | collective-permute-start | bytes 1572872 | tf_op jit(solution)/shard_map/ppermute | solution.py:298
  201.5 52.7 %collective-permute-start.33 = (f32[512,256]{1,0:T(8,128)}, f32[512,256]{1,0:T(8,128)S(1)}, u32[]{:S(2)}, u32[]{:S(2)}) collective-permute-start(f32[512,256]{1,0:T(8,128)} %get-tuple-element.91), channel_id=1, source_target_pairs={{0,64},{16,80},{32,96},{48,112},{64,0},{80,16},{96,32},{112,48},{1... | collective-permute-start | bytes 1572872 | tf_op jit(solution)/shard_map/ppermute | solution.py:298
  204.0 50.2 %collective-permute-start.34 = (f32[512,256]{1,0:T(8,128)S(1)}, f32[512,256]{1,0:T(8,128)S(1)}, u32[]{:S(2)}, u32[]{:S(2)}) collective-permute-start(f32[512,256]{1,0:T(8,128)S(1)} %copy-done.22), channel_id=1, source_target_pairs={{0,80},{16,64},{32,112},{48,96},{64,16},{80,0},{96,48},{112,32},{1... | collective-permute-start | bytes 1572872 | tf_op jit(solution)/shard_map/ppermute | solution.py:298
  204.2 50.0 %copy-start.9 = (f32[512,256]{1,0:T(8,128)}, f32[512,256]{1,0:T(8,128)S(1)}, u32[]{:S(2)}) copy-start(f32[512,256]{1,0:T(8,128)S(1)} %collective-permute-done.30.refs_1_) | copy-start | bytes 1572868
  204.2 50.0 %collective-permute-start.35 = (f32[512,256]{1,0:T(8,128)S(1)}, f32[512,256]{1,0:T(8,128)S(1)}, u32[]{:S(2)}, u32[]{:S(2)}) collective-permute-start(f32[512,256]{1,0:T(8,128)S(1)} %copy-done.21), channel_id=1, source_target_pairs={{0,96},{16,112},{32,0},{48,16},{64,32},{80,48},{96,64},{112,80},{1... | collective-permute-start | bytes 1572872 | tf_op jit(solution)/shard_map/ppermute | solution.py:298
  208.0 46.3 %copy-start.10 = (f32[512,256]{1,0:T(8,128)}, f32[512,256]{1,0:T(8,128)S(1)}, u32[]{:S(2)}) copy-start(f32[512,256]{1,0:T(8,128)S(1)} %collective-permute-done.31.refs_2_) | copy-start | bytes 1572868
  208.0 46.2 %collective-permute-start.36 = (f32[512,256]{1,0:T(8,128)S(1)}, f32[512,256]{1,0:T(8,128)S(1)}, u32[]{:S(2)}, u32[]{:S(2)}) collective-permute-start(f32[512,256]{1,0:T(8,128)S(1)} %copy-done.20), channel_id=1, source_target_pairs={{0,112},{16,96},{32,16},{48,0},{64,48},{80,32},{96,80},{112,64},{1... | collective-permute-start | bytes 1572872 | tf_op jit(solution)/shard_map/ppermute | solution.py:298
  (13 other events, 90.8 us)
where the time goes:
time: 261 us; the launch traced here: 259 us
  waiting for transfers between devices  103 us (39%)
  starting transfers between devices  66 us (25%)
  blocking collectives  43.6 us (17%)
  Pallas kernels  36.7 us (14%)
  other arithmetic  5.29 us (2%)
  local copies, waits for them, and re-layouts  3.81 us (1%)
    ppermute x7, waiting for transfers between devices, per_device(): lax.ppermute(packed[q], 'site', along_site(*order[q]))  49.8 us
    all_to_all x1, blocking collectives, per_device(): lax.all_to_all(reduced, 'site', split_axis=0, concat_axis=0, tiled=True)  43.6 us
    ppermute x4, waiting for transfers between devices, ring_open(): lax.ppermute(down, 'col', perm(-1))  21.7 us
    ppermute x7, starting transfers between devices, per_device(): lax.ppermute(common[q], 'site', along_site(*order[q]))  18.4 us
    ppermute x4, starting transfers between devices, ring_close(): high2 = lax.ppermute(keep3 + from_high[:n], 'col', perm(-1))  15.7 us
    pallas_call x1, Pallas kernels, common_product(): pl.pallas_call(common_body, grid_spec=pltpu.PrefetchScalarGridSpec(num_sc...  10.3 us
    ppermute x4, waiting for transfers between devices, ring_close(): low2 = lax.ppermute(keep1 + from_low[:n], 'col', perm(1))  9.95 us
    pallas_call x1, Pallas kernels, rare_product(): pl.pallas_call(rare_body, in_specs=[pl.BlockSpec(memory_space=pltpu.SMEM)...  9.6 us
  transfers between devices with their start and end apart: 38, of which 14 were waited for; matrix products, arithmetic and copies ran while one was open for 2% of the time, Pallas kernels for 13%

commit v1 on v0

--- a/solution.py
+++ b/solution.py
@@ -195,27 +195,46 @@
     )(places, *slices, *panels)
 
 
-def finish_body(turned_ref, *refs):
-    parts, out_ref = refs[:N_SITE], refs[N_SITE]
-    total = parts[0][...]
-    for part in parts[1:]:
+def sum_body(*refs):
+    total = refs[0][...]
+    for part in refs[1:N_SITE]:
         total = total + part[...]
-    out_ref[...] = (total + turned_ref[...].T) * (1.0 / 8192)
-
-
-def finish(turned, parts):
+    refs[N_SITE][...] = total
+
+
+def sum_parts(parts):
+    rows = PANEL // 4
+    return pl.pallas_call(
+        sum_body,
+        grid=(4,),
+        in_specs=[spec((rows, TILE), lambda i: (i, 0))] * N_SITE,
+        out_specs=spec((rows, TILE), lambda i: (i, 0)),
+        out_shape=jax.ShapeDtypeStruct((PANEL, TILE), F32),
+        compiler_params=pltpu.CompilerParams(vmem_limit_bytes=16 << 20),
+        cost_estimate=pl.CostEstimate(flops=0, bytes_accessed=5 << 20, transcendentals=0),
+        name="sum_parts",
+    )(*parts)
+
+
+def finish_body(turned_ref, common_ref, out_ref):
+    out_ref[...] = (common_ref[...] + turned_ref[...].T) * (1.0 / 8192)
+
+
+def finish(turned, common):
     rows = PANEL // 2
     return pl.pallas_call(
         finish_body,
         grid=(2,),
-        in_specs=[spec((TILE, rows), lambda i: (0, i))]
-        + [spec((rows, TILE), lambda i: (i, 0))] * N_SITE,
+        in_specs=[
+            spec((TILE, rows), lambda i: (0, i)),
+            spec((rows, TILE), lambda i: (i, 0)),
+        ],
         out_specs=spec((rows, TILE), lambda i: (i, 0)),
         out_shape=jax.ShapeDtypeStruct((PANEL, TILE), F32),
-        compiler_params=pltpu.CompilerParams(vmem_limit_bytes=VLIM),
-        cost_estimate=pl.CostEstimate(flops=0, bytes_accessed=6 << 20, transcendentals=0),
+        compiler_params=pltpu.CompilerParams(vmem_limit_bytes=16 << 20),
+        cost_estimate=pl.CostEstimate(flops=0, bytes_accessed=2 << 20, transcendentals=0),
         name="finish",
-    )(turned, *parts)
+    )(turned, common)
 
 
 def along_site(dz, flip):
@@ -246,16 +265,11 @@
     return first, second
 
 
-def ring(up, down, keep1, keep3, own, perm):
-    return ring_close(ring_open(up, down, perm), keep1, keep3, own, perm)
-
-
-def second_ring(first, second, perm):
-    own, one = first[:4], first[4:]
-    two, three = second[:4], second[4:]
-    up = jnp.concatenate([two[:2], one[2:]], axis=0)
-    down = jnp.concatenate([two[2:], three[:2]], axis=0)
-    return ring(up, down, one[:2], three[2:], own, perm)
+def direct(first, second, perm):
+    far = lax.ppermute(second[:4], "col", perm(2))
+    low = lax.ppermute(first[4:], "col", perm(1))
+    high = lax.ppermute(second[4:], "col", perm(-1))
+    return first[:4] + low + high + far
 
 
 def per_device(common_geno, rare_values, block_tile, panel_rare):
@@ -300,11 +314,11 @@
 
     a = ring_close(open_a, *ring_parts[2:5], along_x)
     b = ring_close(open_b, *ring_parts[7:], along_y)
-    a = second_ring(*a, along_y)
-    b = second_ring(*b, along_x)
+    a = direct(*a, along_y)
+    b = direct(*b, along_x)
     reduced = jnp.concatenate([*a, *b], axis=0)
     turned = lax.all_to_all(reduced, "site", split_axis=0, concat_axis=0, tiled=True)
-    return finish(turned.reshape(TILE, PANEL), common)
+    return finish(turned.reshape(TILE, PANEL), sum_parts(common))
 
 
 def solution(mesh):

time: 261 us -> 276 us (1.057)
  blocking collectives: 43.6 us -> 0 us
  waiting for transfers between devices: 103 us -> 146 us
  starting transfers between devices: 66 us -> 79.1 us
    all_to_all x1 -> x0, blocking collectives: 43.6 us -> none  [per_device(): lax.all_to_all(reduced, 'site', split_axis=0, concat_axis=0, tiled=True)]
    ppermute x7, waiting for transfers between devices: 1.78 us -> 36.8 us  [per_device(): lax.ppermute(common[q], 'site', along_site(*order[q]))]
    ppermute x4 -> x2, waiting for transfers between devices: 21.7 us -> 34.4 us  [ring_open(): lax.ppermute(down, 'col', perm(-1))]
    ppermute x0 -> x6, starting transfers between devices: none -> 7.85 us  [the longest x2 3.99 us: direct(): high = lax.ppermute(second[4:], 'col', perm(-1))]
    ppermute x0 -> x6, waiting for transfers between devices: none -> 7.31 us  [the longest x2 6.69 us: direct(): far = lax.ppermute(second[:4], 'col', perm(2))]
    ppermute x4 -> x2, waiting for transfers between devices: 9.95 us -> 3.3 us  [ring_close(): low2 = lax.ppermute(keep1 + from_low[:n], 'col', perm(1))]
    ppermute x4 -> x2, waiting for transfers between devices: 3.69 us -> 0.01 us  [ring_open(): lax.ppermute(up, 'col', perm(1))]
    all_to_all x0 -> x1, starting transfers between devices: none -> 3.44 us  [per_device(): lax.all_to_all(reduced, 'site', split_axis=0, concat_axis=0, tiled=True)]
  transfers between devices with their start and end apart: 38 -> 37, of which waited for: 14 -> 19; matrix products, arithmetic and copies ran while one was open for 2% -> 2% of each run, Pallas kernels for 13% -> 9%
where the time goes in v1:
time: 276 us; the launch traced here: 274 us
  waiting for transfers between devices  146 us (53%)
  starting transfers between devices  79.1 us (29%)
  Pallas kernels  37 us (13%)
  local copies, waits for them, and re-layouts  5.91 us (2%)
  other arithmetic  5.26 us (2%)
    ppermute x7, waiting for transfers between devices, per_device(): lax.ppermute(packed[q], 'site', along_site(*order[q]))  48.1 us
    ppermute x7, waiting for transfers between devices, per_device(): lax.ppermute(common[q], 'site', along_site(*order[q]))  36.8 us
    ppermute x2, waiting for transfers between devices, ring_open(): lax.ppermute(down, 'col', perm(-1))  34.4 us
    ppermute x2, starting transfers between devices, ring_close(): high2 = lax.ppermute(keep3 + from_high[:n], 'col', perm(-1))  18.6 us
    ppermute x7, starting transfers between devices, per_device(): lax.ppermute(common[q], 'site', along_site(*order[q]))  18.2 us
    pallas_call x1, Pallas kernels, common_product(): pl.pallas_call(common_body, grid_spec=pltpu.PrefetchScalarGridSpec(num_sc...  10.3 us
    pallas_call x1, Pallas kernels, rare_product(): pl.pallas_call(rare_body, in_specs=[pl.BlockSpec(memory_space=pltpu.SMEM)...  9.58 us
    ppermute x7, starting transfers between devices, per_device(): lax.ppermute(packed[q], 'site', along_site(*order[q]))  9.09 us
  transfers between devices with their start and end apart: 37, of which 19 were waited for; matrix products, arithmetic and copies ran while one was open for 2% of the time, Pallas kernels for 9%

profile of v1, /device:TPU:1, one launch (start us, length us, event | category | flops | bytes accessed | tf_op | source)
XLA Modules:
  0.0 273.9 jit_solution(13135387887874870835)
XLA Ops:
  0.7 1.1 fusion.1.refs_8_
  1.7 4.6 %collective-permute-start.5 = (bf16[528,512]{1,0:T(8,128)(2,1)S(1)}, bf16[528,512]{1,0:T(8,128)(2,1)S(1)}, u32[]{:S(2)}, u32[]{:S(2)}) collective-permute-start(bf16[528,512]{1,0:T(8,128)(2,1)S(1)} %fusion.1.refs_8_), channel_id=1, source_target_pairs={{0,96},{16,112},{32,0},{48,16},{64,32},{80,48},{96,64},{112,80},{1... | collective-permute-start | bytes 1622024 | tf_op jit(solution)/shard_map/ppermute | solution.py:286
  7.8 5.8 %scale_common.1 = bf16[16,64,2560]{2,1,0:T(8,128)(2,1)} custom-call(bf16[64,32768]{1,0:T(8,128)(2,1)} %x_ref.2), custom_call_target="tpu_custom_call" | custom-call | bytes 9437184 | tf_op jit(solution)/shard_map/scale_common/pallas_call | solution.py:83
  13.6 7.8 %pack_rare.1 = (bf16[512,512]{1,0:T(8,128)(2,1)}, bf16[512,512]{1,0:T(8,128)(2,1)}, bf16[512,512]{1,0:T(8,128)(2,1)}, bf16[512,512]{1,0:T(8,128)(2,1)}, bf16[512...) custom-call(s32[8]{0:T(128)} %broadcast_multiply_fusion.off_ref, ...), custom_call_target="tpu_custom_call" | custom-call | bytes 8388608 | tf_op jit(solution)/shard_map/pack_rare/pallas_call | solution.py:44
  21.4 1.6 collective-permute-start.7
  23.1 5.7 %collective-permute-done.5.refs_14_ = bf16[528,512]{1,0:T(8,128)(2,1)S(1)} collective-permute-done((bf16[528,512]{1,0:T(8,128)(2,1)S(1)}, bf16[528,512]{1,0:T(8,128)(2,1)S(1)}, u32[]{:S(2)}, u32[]{:S(2)}) %collective-permute-start.5) | collective-permute-done | bytes 540704 | tf_op jit(solution)/shard_map/ppermute | solution.py:286
  28.8 1.7 collective-permute-start.6
  30.6 2.5 collective-permute-done.1.refs_10_
  33.9 14.8 %collective-permute-done.8.refs_2_ = bf16[512,512]{1,0:T(8,128)(2,1)S(1)} collective-permute-done((bf16[512,512]{1,0:T(8,128)(2,1)}, bf16[512,512]{1,0:T(8,128)(2,1)S(1)}, u32[]{:S(2)}, u32[]{:S(2)}) %collective-permute-start.8) | collective-permute-done | bytes 524320 | tf_op jit(solution)/shard_map/ppermute | solution.py:297
  48.7 1.4 collective-permute-start.10
  50.1 2.8 %collective-permute-start.11 = (bf16[512,512]{1,0:T(8,128)(2,1)}, bf16[512,512]{1,0:T(8,128)(2,1)}, u32[]{:S(2)}, u32[]{:S(2)}) collective-permute-start(bf16[512,512]{1,0:T(8,128)(2,1)} %get-tuple-element.62), channel_id=1, source_target_pairs={{0,80},{16,64},{32,112},{48,96},{64,16},{80,0},{96,48},{112,32},{1... | collective-permute-start | bytes 1572872 | tf_op jit(solution)/shard_map/ppermute | solution.py:297
  52.9 2.0 collective-permute-start.12
  55.7 1.3 collective-permute-start.13
  57.1 6.8 %all-to-all-start.1 = ((bf16[16,64,2560]{2,1,0:T(8,128)(2,1)}), bf16[16,64,2560]{2,1,0:T(8,128)(2,1)}, u32[]{:S(2)}, u32[]{:S(2)}) async-start(bf16[16,64,2560]{2,1,0:T(8,128)(2,1)} %scale_common.1), calls=%async_computation.1 | async-start | bytes 10485760 | tf_op jit(solution)/shard_map/all_to_all | solution.py:291
  66.1 20.9 %collective-permute-done.9.refs_3_ = bf16[512,512]{1,0:T(8,128)(2,1)} collective-permute-done((bf16[512,512]{1,0:T(8,128)(2,1)}, bf16[512,512]{1,0:T(8,128)(2,1)}, u32[]{:S(2)}, u32[]{:S(2)}) %collective-permute-start.9) | collective-permute-done | bytes 524320 | tf_op jit(solution)/shard_map/ppermute | solution.py:297
  87.0 1.1 collective-permute-done.12.refs_6_
  88.1 11.3 %collective-permute-done.13.refs_7_ = bf16[512,512]{1,0:T(8,128)(2,1)} collective-permute-done((bf16[512,512]{1,0:T(8,128)(2,1)}, bf16[512,512]{1,0:T(8,128)(2,1)}, u32[]{:S(2)}, u32[]{:S(2)}) %collective-permute-start.13) | collective-permute-done | bytes 524320 | tf_op jit(solution)/shard_map/ppermute | solution.py:297
  99.3 9.6 %rare_product.1 = (f32[16,32,512]{2,1,0:T(8,128)}, f32[16,32,512]{2,1,0:T(8,128)}, f32[8,32,512]{2,1,0:T(8,128)}, f32[8,32,512]{2,1,0:T(8,128)}, f32[16,32,512]{...) custom-call(s32[128]{0:T(128)} %fusion.18.place_ref, ...), custom_call_target="tpu_custom_call" | custom-call | flops 2147483648 | bytes 16777216 | tf_op jit(solution)/shard_map/rare_product/pallas_call | solution.py:180
  108.9 2.5 collective-permute-start.14
  111.5 2.7 collective-permute-start.21
  114.2 34.4 %collective-permute-done.14 = f32[16,32,512]{2,1,0:T(8,128)S(1)} collective-permute-done((f32[16,32,512]{2,1,0:T(8,128)}, f32[16,32,512]{2,1,0:T(8,128)S(1)}, u32[]{:S(2)}, u32[]{:S(2)}) %collective-permute-start.14) | collective-permute-done | bytes 1048608 | tf_op jit(solution)/shard_map/ppermute | solution.py:255
  148.6 1.1 slice_add_fusion.4
  149.7 18.5 %collective-permute-start.18 = (f32[8,32,512]{2,1,0:T(8,128)S(1)}, f32[8,32,512]{2,1,0:T(8,128)S(1)}, u32[]{:S(2)}, u32[]{:S(2)}) collective-permute-start(f32[8,32,512]{2,1,0:T(8,128)S(1)} %slice_add_fusion.4), channel_id=1, source_target_pairs={{0,12},{1,13},{2,14},{3,15},{4,0},{5,1},{6,2},{7,3},{8,4},{9,5},{1... | collective-permute-start | bytes 1572872 | tf_op jit(solution)/shard_map/ppermute | solution.py:262
  169.5 1.7 collective-permute-start.23
  171.2 7.4 %collective-permute-done.18 = f32[8,32,512]{2,1,0:T(8,128)S(1)} collective-permute-done((f32[8,32,512]{2,1,0:T(8,128)S(1)}, f32[8,32,512]{2,1,0:T(8,128)S(1)}, u32[]{:S(2)}, u32[]{:S(2)}) %collective-permute-start.18) | collective-permute-done | bytes 524320 | tf_op jit(solution)/shard_map/ppermute | solution.py:262
  178.5 3.3 %collective-permute-done.16 = f32[8,32,512]{2,1,0:T(8,128)S(1)} collective-permute-done((f32[8,32,512]{2,1,0:T(8,128)S(1)}, f32[8,32,512]{2,1,0:T(8,128)S(1)}, u32[]{:S(2)}, u32[]{:S(2)}) %collective-permute-start.16) | collective-permute-done | bytes 524320 | tf_op jit(solution)/shard_map/ppermute | solution.py:261
  182.3 1.5 collective-permute-start.17
  183.8 1.3 collective-permute-start.19
  186.3 2.7 collective-permute-start.26
  189.3 1.6 collective-permute-start.27
  190.9 2.9 %collective-permute-done.20 = f32[4,32,512]{2,1,0:T(8,128)S(1)} collective-permute-done((f32[4,32,512]{2,1,0:T(8,128)S(1)}, f32[4,32,512]{2,1,0:T(8,128)S(1)}, u32[]{:S(2)}, u32[]{:S(2)}) %collective-permute-start.20) | collective-permute-done | bytes 262176 | tf_op jit(solution)/shard_map/ppermute | solution.py:269
  194.4 3.7 %collective-permute-done.27 = f32[4,32,512]{2,1,0:T(8,128)S(1)} collective-permute-done((f32[4,32,512]{2,1,0:T(8,128)S(1)}, f32[4,32,512]{2,1,0:T(8,128)S(1)}, u32[]{:S(2)}, u32[]{:S(2)}) %collective-permute-start.27) | collective-permute-done | bytes 262176 | tf_op jit(solution)/shard_map/ppermute | solution.py:269
  198.2 10.3 %common_product.1 = (f32[512,256]{1,0:T(8,128)}, f32[512,256]{1,0:T(8,128)}, f32[512,256]{1,0:T(8,128)}, f32[512,256]{1,0:T(8,128)}, f32[512,256]{1,0:T(8,128)},...) custom-call(s32[8]{0:T(128)} %copy-done.20, bf16[1024,2560]{1,0:T(8,128)(2,1)} %bitcast.19.panel_ref.owned_ref, ...), custom_call_target="tpu_custom_call" | custom-call | flops 2147483648 | bytes 9437184 | tf_op jit(solution)/shard_map/common_product/pallas_call | solution.py:115
  208.5 7.7 %collective-permute-start.28 = (f32[512,256]{1,0:T(8,128)}, f32[512,256]{1,0:T(8,128)S(1)}, u32[]{:S(2)}, u32[]{:S(2)}) collective-permute-start(f32[512,256]{1,0:T(8,128)} %get-tuple-element.88), channel_id=1, source_target_pairs={{0,16},{16,0},{32,48},{48,32},{64,80},{80,64},{96,112},{112,96},{1... | collective-permute-start | bytes 1572872 | tf_op jit(solution)/shard_map/ppermute | solution.py:312
  216.2 1.8 collective-permute-start.29
  218.0 0.9 collective-permute-start.30
  218.9 2.7 collective-permute-start.31
  222.2 2.1 collective-permute-start.33
  224.3 8.3 %collective-permute-done.29.refs_2_ = f32[512,256]{1,0:T(8,128)S(1)} collective-permute-done((f32[512,256]{1,0:T(8,128)}, f32[512,256]{1,0:T(8,128)S(1)}, u32[]{:S(2)}, u32[]{:S(2)}) %collective-permute-start.29) | collective-permute-done | bytes 524320 | tf_op jit(solution)/shard_map/ppermute | solution.py:312
  232.6 2.5 collective-permute-start.34
  235.9 3.4 %all-to-all-start = ((f32[8,32,512]{2,1,0:T(8,128)}), f32[8,32,512]{2,1,0:T(8,128)S(1)}, u32[]{:S(2)}, u32[]{:S(2)}) async-start(f32[8,32,512]{2,1,0:T(8,128)} %bitcast.46), calls=%async_computation | async-start | bytes 1048576 | tf_op jit(solution)/shard_map/all_to_all | solution.py:320
  239.4 4.7 %collective-permute-done.30.refs_3_ = f32[512,256]{1,0:T(8,128)S(1)} collective-permute-done((f32[512,256]{1,0:T(8,128)}, f32[512,256]{1,0:T(8,128)S(1)}, u32[]{:S(2)}, u32[]{:S(2)}) %collective-permute-start.30) | collective-permute-done | bytes 524320 | tf_op jit(solution)/shard_map/ppermute | solution.py:312
  244.0 12.0 %collective-permute-done.31.refs_4_ = f32[512,256]{1,0:T(8,128)S(1)} collective-permute-done((f32[512,256]{1,0:T(8,128)}, f32[512,256]{1,0:T(8,128)S(1)}, u32[]{:S(2)}, u32[]{:S(2)}) %collective-permute-start.31) | collective-permute-done | bytes 524320 | tf_op jit(solution)/shard_map/ppermute | solution.py:312
  256.8 11.5 %collective-permute-done.32.refs_5_ = f32[512,256]{1,0:T(8,128)} collective-permute-done((f32[512,256]{1,0:T(8,128)}, f32[512,256]{1,0:T(8,128)}, u32[]{:S(2)}, u32[]{:S(2)}) %collective-permute-start.32) | collective-permute-done | bytes 524320 | tf_op jit(solution)/shard_map/ppermute | solution.py:312
  268.6 1.0 copy-done.2
  269.7 2.4 sum_parts.1.common_ref
  272.1 0.8 all-to-all-done
  272.9 1.0 finish.1
  (109 shorter events, 12.0 us)
Async XLA Ops:
  1.7 21.3 %copy-start.3 = (bf16[528,512]{1,0:T(8,128)(2,1)}, bf16[528,512]{1,0:T(8,128)(2,1)S(1)}, u32[]{:S(2)}) copy-start(bf16[528,512]{1,0:T(8,128)(2,1)S(1)} %fusion.1.refs_8_) | copy-start | bytes 1622020
  1.7 27.0 %collective-permute-start.5 = (bf16[528,512]{1,0:T(8,128)(2,1)S(1)}, bf16[528,512]{1,0:T(8,128)(2,1)S(1)}, u32[]{:S(2)}, u32[]{:S(2)}) collective-permute-start(bf16[528,512]{1,0:T(8,128)(2,1)S(1)} %fusion.1.refs_8_), channel_id=1, source_target_pairs={{0,96},{16,112},{32,0},{48,16},{64,32},{80,48},{96,64},{112,80},{1... | collective-permute-start | bytes 1622024 | tf_op jit(solution)/shard_map/ppermute | solution.py:286
  6.4 24.1 %collective-permute-start.3 = (bf16[528,512]{1,0:T(8,128)(2,1)S(1)}, bf16[528,512]{1,0:T(8,128)(2,1)S(1)}, u32[]{:S(2)}, u32[]{:S(2)}) collective-permute-start(bf16[528,512]{1,0:T(8,128)(2,1)S(1)} %fusion.1.refs_8_), channel_id=1, source_target_pairs={{0,64},{16,80},{32,96},{48,112},{64,0},{80,16},{96,32},{112,48},{1... | collective-permute-start | bytes 1622024 | tf_op jit(solution)/shard_map/ppermute | solution.py:286
  6.4 26.7 %collective-permute-start.1 = (bf16[528,512]{1,0:T(8,128)(2,1)S(1)}, bf16[528,512]{1,0:T(8,128)(2,1)S(1)}, u32[]{:S(2)}, u32[]{:S(2)}) collective-permute-start(bf16[528,512]{1,0:T(8,128)(2,1)S(1)} %fusion.1.refs_8_), channel_id=1, source_target_pairs={{0,32},{16,48},{32,64},{48,80},{64,96},{80,112},{96,0},{112,16},{1... | collective-permute-start | bytes 1622024 | tf_op jit(solution)/shard_map/ppermute | solution.py:286
  21.4 12.4 %collective-permute-start.7 = (bf16[512,512]{1,0:T(8,128)(2,1)}, bf16[512,512]{1,0:T(8,128)(2,1)S(1)}, u32[]{:S(2)}, u32[]{:S(2)}) collective-permute-start(bf16[512,512]{1,0:T(8,128)(2,1)} %get-tuple-element.58), channel_id=1, source_target_pairs={{0,16},{16,0},{32,48},{48,32},{64,80},{80,64},{96,112},{112,96},{1... | collective-permute-start | bytes 1572872 | tf_op jit(solution)/shard_map/ppermute | solution.py:297
  23.0 25.7 %collective-permute-start = (bf16[528,512]{1,0:T(8,128)(2,1)S(1)}, bf16[528,512]{1,0:T(8,128)(2,1)S(1)}, u32[]{:S(2)}, u32[]{:S(2)}) collective-permute-start(bf16[528,512]{1,0:T(8,128)(2,1)S(1)} %fusion.1.refs_8_), channel_id=1, source_target_pairs={{0,16},{16,0},{32,48},{48,32},{64,80},{80,64},{96,112},{112,96},{1... | collective-permute-start | bytes 1622024 | tf_op jit(solution)/shard_map/ppermute | solution.py:294
  28.8 35.1 %copy-start.7 = (bf16[528,512]{1,0:T(8,128)(2,1)}, bf16[528,512]{1,0:T(8,128)(2,1)S(1)}, u32[]{:S(2)}) copy-start(bf16[528,512]{1,0:T(8,128)(2,1)S(1)} %collective-permute-done.5.refs_14_) | copy-start | bytes 1622020
  28.8 21.3 %collective-permute-start.6 = (bf16[528,512]{1,0:T(8,128)(2,1)S(1)}, bf16[528,512]{1,0:T(8,128)(2,1)S(1)}, u32[]{:S(2)}, u32[]{:S(2)}) collective-permute-start(bf16[528,512]{1,0:T(8,128)(2,1)S(1)} %collective-permute-done.5.refs_14_), channel_id=1, source_target_pairs={{0,16},{16,0},{32,48},{48,32},{64,80},{80,64},{96,112},{112,96},{1... | collective-permute-start | bytes 1622024 | tf_op jit(solution)/shard_map/ppermute | solution.py:294
  30.5 33.4 %copy-start.8 = (bf16[528,512]{1,0:T(8,128)(2,1)}, bf16[528,512]{1,0:T(8,128)(2,1)S(1)}, u32[]{:S(2)}) copy-start(bf16[528,512]{1,0:T(8,128)(2,1)S(1)} %collective-permute-done.3.refs_12_) | copy-start | bytes 1622020
  30.5 22.4 %collective-permute-start.4 = (bf16[528,512]{1,0:T(8,128)(2,1)S(1)}, bf16[528,512]{1,0:T(8,128)(2,1)S(1)}, u32[]{:S(2)}, u32[]{:S(2)}) collective-permute-start(bf16[528,512]{1,0:T(8,128)(2,1)S(1)} %collective-permute-done.3.refs_12_), channel_id=1, source_target_pairs={{0,16},{16,0},{32,48},{48,32},{64,80},{80,64},{96,112},{112,96},{1... | collective-permute-start | bytes 1622024 | tf_op jit(solution)/shard_map/ppermute | solution.py:294
  33.1 30.8 %copy-start.9 = (bf16[528,512]{1,0:T(8,128)(2,1)}, bf16[528,512]{1,0:T(8,128)(2,1)S(1)}, u32[]{:S(2)}) copy-start(bf16[528,512]{1,0:T(8,128)(2,1)S(1)} %collective-permute-done.1.refs_10_) | copy-start | bytes 1622020
  33.1 21.8 %collective-permute-start.2 = (bf16[528,512]{1,0:T(8,128)(2,1)S(1)}, bf16[528,512]{1,0:T(8,128)(2,1)S(1)}, u32[]{:S(2)}, u32[]{:S(2)}) collective-permute-start(bf16[528,512]{1,0:T(8,128)(2,1)S(1)} %collective-permute-done.1.refs_10_), channel_id=1, source_target_pairs={{0,16},{16,0},{32,48},{48,32},{64,80},{80,64},{96,112},{112,96},{1... | collective-permute-start | bytes 1622024 | tf_op jit(solution)/shard_map/ppermute | solution.py:294
  33.9 21.1 %copy-start.14 = (bf16[512,512]{1,0:T(8,128)(2,1)}, bf16[512,512]{1,0:T(8,128)(2,1)S(1)}, u32[]{:S(2)}) copy-start(bf16[512,512]{1,0:T(8,128)(2,1)S(1)} %collective-permute-done.7.refs_1_) | copy-start | bytes 1572868
  33.9 14.8 %collective-permute-start.8 = (bf16[512,512]{1,0:T(8,128)(2,1)}, bf16[512,512]{1,0:T(8,128)(2,1)S(1)}, u32[]{:S(2)}, u32[]{:S(2)}) collective-permute-start(bf16[512,512]{1,0:T(8,128)(2,1)} %get-tuple-element.59), channel_id=1, source_target_pairs={{0,32},{16,48},{32,64},{48,80},{64,96},{80,112},{96,0},{112,16},{1... | collective-permute-start | bytes 1572872 | tf_op jit(solution)/shard_map/ppermute | solution.py:297
  48.7 38.3 %collective-permute-start.9 = (bf16[512,512]{1,0:T(8,128)(2,1)}, bf16[512,512]{1,0:T(8,128)(2,1)}, u32[]{:S(2)}, u32[]{:S(2)}) collective-permute-start(bf16[512,512]{1,0:T(8,128)(2,1)} %get-tuple-element.60), channel_id=1, source_target_pairs={{0,48},{16,32},{32,80},{48,64},{64,112},{80,96},{96,16},{112,0},{1... | collective-permute-start | bytes 1572872 | tf_op jit(solution)/shard_map/ppermute | solution.py:297
  48.7 15.2 %copy-start.10 = (bf16[528,512]{1,0:T(8,128)(2,1)}, bf16[528,512]{1,0:T(8,128)(2,1)S(1)}, u32[]{:S(2)}) copy-start(bf16[528,512]{1,0:T(8,128)(2,1)S(1)} %collective-permute-done.refs_9_) | copy-start | bytes 1622020
  48.7 38.2 %collective-permute-start.10 = (bf16[512,512]{1,0:T(8,128)(2,1)}, bf16[512,512]{1,0:T(8,128)(2,1)S(1)}, u32[]{:S(2)}, u32[]{:S(2)}) collective-permute-start(bf16[512,512]{1,0:T(8,128)(2,1)} %get-tuple-element.61), channel_id=1, source_target_pairs={{0,64},{16,80},{32,96},{48,112},{64,0},{80,16},{96,32},{112,48},{1... | collective-permute-start | bytes 1572872 | tf_op jit(solution)/shard_map/ppermute | solution.py:297
  50.1 13.8 %copy-start.11 = (bf16[528,512]{1,0:T(8,128)(2,1)}, bf16[528,512]{1,0:T(8,128)(2,1)S(1)}, u32[]{:S(2)}) copy-start(bf16[528,512]{1,0:T(8,128)(2,1)S(1)} %collective-permute-done.6.refs_15_) | copy-start | bytes 1622020
  50.1 36.8 %collective-permute-start.11 = (bf16[512,512]{1,0:T(8,128)(2,1)}, bf16[512,512]{1,0:T(8,128)(2,1)}, u32[]{:S(2)}, u32[]{:S(2)}) collective-permute-start(bf16[512,512]{1,0:T(8,128)(2,1)} %get-tuple-element.62), channel_id=1, source_target_pairs={{0,80},{16,64},{32,112},{48,96},{64,16},{80,0},{96,48},{112,32},{1... | collective-permute-start | bytes 1572872 | tf_op jit(solution)/shard_map/ppermute | solution.py:297
  52.9 35.2 %collective-permute-start.12 = (bf16[512,512]{1,0:T(8,128)(2,1)}, bf16[512,512]{1,0:T(8,128)(2,1)}, u32[]{:S(2)}, u32[]{:S(2)}) collective-permute-start(bf16[512,512]{1,0:T(8,128)(2,1)} %get-tuple-element.63), channel_id=1, source_target_pairs={{0,96},{16,112},{32,0},{48,16},{64,32},{80,48},{96,64},{112,80},{1... | collective-permute-start | bytes 1572872 | tf_op jit(solution)/shard_map/ppermute | solution.py:297
  55.7 43.6 %collective-permute-start.13 = (bf16[512,512]{1,0:T(8,128)(2,1)}, bf16[512,512]{1,0:T(8,128)(2,1)}, u32[]{:S(2)}, u32[]{:S(2)}) collective-permute-start(bf16[512,512]{1,0:T(8,128)(2,1)} %get-tuple-element.64), channel_id=1, source_target_pairs={{0,112},{16,96},{32,16},{48,0},{64,48},{80,32},{96,80},{112,64},{1... | collective-permute-start | bytes 1572872 | tf_op jit(solution)/shard_map/ppermute | solution.py:297
  57.1 141.1 %all-to-all-start.1 = ((bf16[16,64,2560]{2,1,0:T(8,128)(2,1)}), bf16[16,64,2560]{2,1,0:T(8,128)(2,1)}, u32[]{:S(2)}, u32[]{:S(2)}) async-start(bf16[16,64,2560]{2,1,0:T(8,128)(2,1)} %scale_common.1), calls=%async_computation.1 | async-start | bytes 10485760 | tf_op jit(solution)/shard_map/all_to_all | solution.py:291
  108.9 59.3 %copy-start.19 = (f32[8,32,512]{2,1,0:T(8,128)S(1)}, f32[8,32,512]{2,1,0:T(8,128)}, u32[]{:S(2)}) copy-start(f32[8,32,512]{2,1,0:T(8,128)} %get-tuple-element.77) | copy-start | bytes 1572868
  108.9 39.7 %collective-permute-start.14 = (f32[16,32,512]{2,1,0:T(8,128)}, f32[16,32,512]{2,1,0:T(8,128)S(1)}, u32[]{:S(2)}, u32[]{:S(2)}) collective-permute-start(f32[16,32,512]{2,1,0:T(8,128)} %get-tuple-element.76), channel_id=1, source_target_pairs={{0,12},{1,13},{2,14},{3,15},{4,0},{5,1},{6,2},{7,3},{8,4},{9,5},{1... | collective-permute-start | bytes 3145736 | tf_op jit(solution)/shard_map/ppermute | solution.py:255
  111.5 56.8 %collective-permute-start.15 = (f32[16,32,512]{2,1,0:T(8,128)}, f32[16,32,512]{2,1,0:T(8,128)S(1)}, u32[]{:S(2)}, u32[]{:S(2)}) collective-permute-start(f32[16,32,512]{2,1,0:T(8,128)} %get-tuple-element.78), channel_id=1, source_target_pairs={{0,4},{1,5},{2,6},{3,7},{4,8},{5,9},{6,10},{7,11},{8,12},{9,13},{1... | collective-permute-start | bytes 3145736 | tf_op jit(solution)/shard_map/ppermute | solution.py:255
  111.5 56.9 %collective-permute-start.21 = (f32[16,32,512]{2,1,0:T(8,128)}, f32[16,32,512]{2,1,0:T(8,128)S(1)}, u32[]{:S(2)}, u32[]{:S(2)}) collective-permute-start(f32[16,32,512]{2,1,0:T(8,128)} %get-tuple-element.81), channel_id=1, source_target_pairs={{0,3},{1,0},{2,1},{3,2},{4,7},{5,4},{6,5},{7,6},{8,11},{9,8},{10,9... | collective-permute-start | bytes 3145736 | tf_op jit(solution)/shard_map/ppermute | solution.py:255
  114.2 54.4 %collective-permute-start.22 = (f32[16,32,512]{2,1,0:T(8,128)}, f32[16,32,512]{2,1,0:T(8,128)S(1)}, u32[]{:S(2)}, u32[]{:S(2)}) collective-permute-start(f32[16,32,512]{2,1,0:T(8,128)} %get-tuple-element.83), channel_id=1, source_target_pairs={{0,1},{1,2},{2,3},{3,0},{4,5},{5,6},{6,7},{7,4},{8,9},{9,10},{10,1... | collective-permute-start | bytes 3145736 | tf_op jit(solution)/shard_map/ppermute | solution.py:255
  149.7 18.7 %copy-start.18 = (f32[8,32,512]{2,1,0:T(8,128)S(1)}, f32[8,32,512]{2,1,0:T(8,128)}, u32[]{:S(2)}) copy-start(f32[8,32,512]{2,1,0:T(8,128)} %get-tuple-element.84) | copy-start | bytes 1572868
  149.7 28.8 %collective-permute-start.18 = (f32[8,32,512]{2,1,0:T(8,128)S(1)}, f32[8,32,512]{2,1,0:T(8,128)S(1)}, u32[]{:S(2)}, u32[]{:S(2)}) collective-permute-start(f32[8,32,512]{2,1,0:T(8,128)S(1)} %slice_add_fusion.4), channel_id=1, source_target_pairs={{0,12},{1,13},{2,14},{3,15},{4,0},{5,1},{6,2},{7,3},{8,4},{9,5},{1... | collective-permute-start | bytes 1572872 | tf_op jit(solution)/shard_map/ppermute | solution.py:262
  168.3 13.5 %collective-permute-start.16 = (f32[8,32,512]{2,1,0:T(8,128)S(1)}, f32[8,32,512]{2,1,0:T(8,128)S(1)}, u32[]{:S(2)}, u32[]{:S(2)}) collective-permute-start(f32[8,32,512]{2,1,0:T(8,128)S(1)} %slice_add_fusion.6), channel_id=1, source_target_pairs={{0,4},{1,5},{2,6},{3,7},{4,8},{5,9},{6,10},{7,11},{8,12},{9,13},{1... | collective-permute-start | bytes 1572872 | tf_op jit(solution)/shard_map/ppermute | solution.py:261
  168.5 13.3 %copy-start.5 = (f32[16,32,512]{2,1,0:T(8,128)S(1)}, f32[16,32,512]{2,1,0:T(8,128)}, u32[]{:S(2)}) copy-start(f32[16,32,512]{2,1,0:T(8,128)} %get-tuple-element.75) | copy-start | bytes 3145732
  168.5 17.2 %collective-permute-start.25 = (f32[8,32,512]{2,1,0:T(8,128)S(1)}, f32[8,32,512]{2,1,0:T(8,128)S(1)}, u32[]{:S(2)}, u32[]{:S(2)}) collective-permute-start(f32[8,32,512]{2,1,0:T(8,128)S(1)} %slice_add_fusion), channel_id=1, source_target_pairs={{0,3},{1,0},{2,1},{3,2},{4,7},{5,4},{6,5},{7,6},{8,11},{9,8},{10,9... | collective-permute-start | bytes 1572872 | tf_op jit(solution)/shard_map/ppermute | solution.py:262
  169.5 16.3 %collective-permute-start.23 = (f32[8,32,512]{2,1,0:T(8,128)S(1)}, f32[8,32,512]{2,1,0:T(8,128)S(1)}, u32[]{:S(2)}, u32[]{:S(2)}) collective-permute-start(f32[8,32,512]{2,1,0:T(8,128)S(1)} %slice_add_fusion.2), channel_id=1, source_target_pairs={{0,1},{1,2},{2,3},{3,0},{4,5},{5,6},{6,7},{7,4},{8,9},{9,10},{10,1... | collective-permute-start | bytes 1572872 | tf_op jit(solution)/shard_map/ppermute | solution.py:261
  182.3 7.0 %collective-permute-start.17 = (f32[4,32,512]{2,1,0:T(8,128)S(1)}, f32[4,32,512]{2,1,0:T(8,128)S(1)}, u32[]{:S(2)}, u32[]{:S(2)}) collective-permute-start(f32[4,32,512]{2,1,0:T(8,128)S(1)} %slice.138), channel_id=1, source_target_pairs={{0,1},{1,2},{2,3},{3,0},{4,5},{5,6},{6,7},{7,4},{8,9},{9,10},{10,1... | collective-permute-start | bytes 786440 | tf_op jit(solution)/shard_map/ppermute | solution.py:270
  183.8 7.1 %collective-permute-start.19 = (f32[4,32,512]{2,1,0:T(8,128)S(1)}, f32[4,32,512]{2,1,0:T(8,128)S(1)}, u32[]{:S(2)}, u32[]{:S(2)}) collective-permute-start(f32[4,32,512]{2,1,0:T(8,128)S(1)} %get-tuple-element.101), channel_id=1, source_target_pairs={{0,3},{1,0},{2,1},{3,2},{4,7},{5,4},{6,5},{7,6},{8,11},{9,8},{10,9... | collective-permute-start | bytes 786440 | tf_op jit(solution)/shard_map/ppermute | solution.py:271
  185.1 8.7 %collective-permute-start.20 = (f32[4,32,512]{2,1,0:T(8,128)S(1)}, f32[4,32,512]{2,1,0:T(8,128)S(1)}, u32[]{:S(2)}, u32[]{:S(2)}) collective-permute-start(f32[4,32,512]{2,1,0:T(8,128)S(1)} %get-tuple-element.102), channel_id=1, source_target_pairs={{0,2},{1,3},{2,0},{3,1},{4,6},{5,7},{6,4},{7,5},{8,10},{9,11},{10,... | collective-permute-start | bytes 786440 | tf_op jit(solution)/shard_map/ppermute | solution.py:269
  186.2 7.8 %collective-permute-start.24 = (f32[4,32,512]{2,1,0:T(8,128)S(1)}, f32[4,32,512]{2,1,0:T(8,128)S(1)}, u32[]{:S(2)}, u32[]{:S(2)}) collective-permute-start(f32[4,32,512]{2,1,0:T(8,128)S(1)} %slice.146), channel_id=1, source_target_pairs={{0,4},{1,5},{2,6},{3,7},{4,8},{5,9},{6,10},{7,11},{8,12},{9,13},{1... | collective-permute-start | bytes 786440 | tf_op jit(solution)/shard_map/ppermute | solution.py:270
  186.3 8.1 %collective-permute-start.26 = (f32[4,32,512]{2,1,0:T(8,128)S(1)}, f32[4,32,512]{2,1,0:T(8,128)S(1)}, u32[]{:S(2)}, u32[]{:S(2)}) collective-permute-start(f32[4,32,512]{2,1,0:T(8,128)S(1)} %get-tuple-element.99), channel_id=1, source_target_pairs={{0,12},{1,13},{2,14},{3,15},{4,0},{5,1},{6,2},{7,3},{8,4},{9,5},{1... | collective-permute-start | bytes 786440 | tf_op jit(solution)/shard_map/ppermute | solution.py:271
  189.3 8.8 %collective-permute-start.27 = (f32[4,32,512]{2,1,0:T(8,128)S(1)}, f32[4,32,512]{2,1,0:T(8,128)S(1)}, u32[]{:S(2)}, u32[]{:S(2)}) collective-permute-start(f32[4,32,512]{2,1,0:T(8,128)S(1)} %get-tuple-element.100), channel_id=1, source_target_pairs={{0,8},{1,9},{2,10},{3,11},{4,12},{5,13},{6,14},{7,15},{8,0},{9,1},... | collective-permute-start | bytes 786440 | tf_op jit(solution)/shard_map/ppermute | solution.py:269
  208.5 60.1 %copy-start = (f32[512,256]{1,0:T(8,128)S(1)}, f32[512,256]{1,0:T(8,128)}, u32[]{:S(2)}) copy-start(f32[512,256]{1,0:T(8,128)} %get-tuple-element.87.refs_0_) | copy-start | bytes 1572868
  208.5 13.6 %collective-permute-start.28 = (f32[512,256]{1,0:T(8,128)}, f32[512,256]{1,0:T(8,128)S(1)}, u32[]{:S(2)}, u32[]{:S(2)}) collective-permute-start(f32[512,256]{1,0:T(8,128)} %get-tuple-element.88), channel_id=1, source_target_pairs={{0,16},{16,0},{32,48},{48,32},{64,80},{80,64},{96,112},{112,96},{1... | collective-permute-start | bytes 1572872 | tf_op jit(solution)/shard_map/ppermute | solution.py:312
  216.2 16.4 %collective-permute-start.29 = (f32[512,256]{1,0:T(8,128)}, f32[512,256]{1,0:T(8,128)S(1)}, u32[]{:S(2)}, u32[]{:S(2)}) collective-permute-start(f32[512,256]{1,0:T(8,128)} %get-tuple-element.89), channel_id=1, source_target_pairs={{0,32},{16,48},{32,64},{48,80},{64,96},{80,112},{96,0},{112,16},{1... | collective-permute-start | bytes 1572872 | tf_op jit(solution)/shard_map/ppermute | solution.py:312
  218.0 26.0 %collective-permute-start.30 = (f32[512,256]{1,0:T(8,128)}, f32[512,256]{1,0:T(8,128)S(1)}, u32[]{:S(2)}, u32[]{:S(2)}) collective-permute-start(f32[512,256]{1,0:T(8,128)} %get-tuple-element.90), channel_id=1, source_target_pairs={{0,48},{16,32},{32,80},{48,64},{64,112},{80,96},{96,16},{112,0},{1... | collective-permute-start | bytes 1572872 | tf_op jit(solution)/shard_map/ppermute | solution.py:312
  218.9 37.1 %collective-permute-start.31 = (f32[512,256]{1,0:T(8,128)}, f32[512,256]{1,0:T(8,128)S(1)}, u32[]{:S(2)}, u32[]{:S(2)}) collective-permute-start(f32[512,256]{1,0:T(8,128)} %get-tuple-element.91), channel_id=1, source_target_pairs={{0,64},{16,80},{32,96},{48,112},{64,0},{80,16},{96,32},{112,48},{1... | collective-permute-start | bytes 1572872 | tf_op jit(solution)/shard_map/ppermute | solution.py:312
  221.5 46.8 %collective-permute-start.32 = (f32[512,256]{1,0:T(8,128)}, f32[512,256]{1,0:T(8,128)}, u32[]{:S(2)}, u32[]{:S(2)}) collective-permute-start(f32[512,256]{1,0:T(8,128)} %get-tuple-element.92), channel_id=1, source_target_pairs={{0,80},{16,64},{32,112},{48,96},{64,16},{80,0},{96,48},{112,32},{1... | collective-permute-start | bytes 1572872 | tf_op jit(solution)/shard_map/ppermute | solution.py:312
  222.2 46.2 %collective-permute-start.33 = (f32[512,256]{1,0:T(8,128)}, f32[512,256]{1,0:T(8,128)}, u32[]{:S(2)}, u32[]{:S(2)}) collective-permute-start(f32[512,256]{1,0:T(8,128)} %get-tuple-element.93), channel_id=1, source_target_pairs={{0,96},{16,112},{32,0},{48,16},{64,32},{80,48},{96,64},{112,80},{1... | collective-permute-start | bytes 1572872 | tf_op jit(solution)/shard_map/ppermute | solution.py:312
  232.6 36.0 %collective-permute-start.34 = (f32[512,256]{1,0:T(8,128)}, f32[512,256]{1,0:T(8,128)}, u32[]{:S(2)}, u32[]{:S(2)}) collective-permute-start(f32[512,256]{1,0:T(8,128)} %get-tuple-element.94), channel_id=1, source_target_pairs={{0,112},{16,96},{32,16},{48,0},{64,48},{80,32},{96,80},{112,64},{1... | collective-permute-start | bytes 1572872 | tf_op jit(solution)/shard_map/ppermute | solution.py:312
  235.9 36.9 %all-to-all-start = ((f32[8,32,512]{2,1,0:T(8,128)}), f32[8,32,512]{2,1,0:T(8,128)S(1)}, u32[]{:S(2)}, u32[]{:S(2)}) async-start(f32[8,32,512]{2,1,0:T(8,128)} %bitcast.46), calls=%async_computation | async-start | bytes 1048576 | tf_op jit(solution)/shard_map/all_to_all | solution.py:320
  (10 other events, 35.0 us)

commit v2 on v1

v2 whole, which is shorter than its diff:
```python
import jax
import jax.numpy as jnp
from jax import lax
from jax.experimental import pallas as pl
from jax.experimental.pallas import tpu as pltpu
from jax.sharding import PartitionSpec as P


epsilon = 1e-05
BF = jnp.bfloat16
F32 = jnp.float32
NX = 4
NY = 4
NZ = 4
N_SITE = 8
N_COL = 16
TILE = 256
PANEL = 512
SBLK = 512
BLKS = 16
SLICE = TILE // N_SITE
VLIM = 24 * 1024 * 1024
WIDE = 60 * 1024 * 1024


def spec(shape, index_map):
    return pl.BlockSpec(shape, index_map)


def whole_vmem():
    return pl.BlockSpec(memory_space=pltpu.VMEM)


def pack_body(off_ref, x_ref, *rest):
    outs, turned = rest[:N_SITE], rest[N_SITE]
    for b in range(x_ref.shape[0]):
        turned[...] = x_ref[b].T
        for q in range(N_SITE):
            start = pl.multiple_of(off_ref[q], SLICE)
            outs[q][b * SLICE : (b + 1) * SLICE, :] = turned[pl.ds(start, SLICE), :]


def pack(rare_values, offsets):
    per = 2
    return pl.pallas_call(
        pack_body,
        grid_spec=pltpu.PrefetchScalarGridSpec(
            num_scalar_prefetch=1,
            grid=(BLKS // per,),
            in_specs=[spec((per, SBLK, TILE), lambda k, off: (k, 0, 0))],
            out_specs=[spec((per * SLICE, SBLK), lambda k, off: (k, 0))] * N_SITE,
            scratch_shapes=[pltpu.VMEM((TILE, SBLK), BF)],
        ),
        out_shape=[jax.ShapeDtypeStruct((BLKS * SLICE, SBLK), BF)] * N_SITE,
        compiler_params=pltpu.CompilerParams(vmem_limit_bytes=WIDE),
        cost_estimate=pl.CostEstimate(flops=0, bytes_accessed=8 << 20, transcendentals=0),
        name="pack_rare",
    )(offsets, rare_values)


def scale_body(x_ref, out_ref, panel_ref):
    rows, samples = x_ref.shape
    tiles = samples // TILE
    total = jnp.zeros((rows, TILE), F32)
    for t in range(tiles):
        total = total + x_ref[:, t * TILE : (t + 1) * TILE].astype(F32)
    freq = jnp.sum(total, axis=1, keepdims=True) / (2.0 * samples)
    scaling = lax.rsqrt(2.0 * freq * (1.0 - freq) + epsilon)
    mean = 2.0 * freq
    for t in range(tiles):
        scaled = ((x_ref[:, t * TILE : (t + 1) * TILE].astype(F32) - mean) * scaling).astype(BF)
        at = t // N_COL * TILE
        out_ref[t % N_COL, :, at : at + TILE] = scaled
        if t < PANEL // TILE:
            panel_ref[:, t * TILE : (t + 1) * TILE] = scaled


def scale(common_geno):
    sites, samples = common_geno.shape
    rows = 16
    width = samples // N_COL
    return pl.pallas_call(
        scale_body,
        grid=(sites // rows,),
        in_specs=[spec((rows, samples), lambda i: (i, 0))],
        out_specs=[
            spec((N_COL, rows, width), lambda i: (0, i, 0)),
            spec((rows, PANEL), lambda i: (i, 0)),
        ],
        out_shape=[
            jax.ShapeDtypeStruct((N_COL, sites, width), BF),
            jax.ShapeDtypeStruct((sites, PANEL), BF),
        ],
        compiler_params=pltpu.CompilerParams(vmem_limit_bytes=WIDE),
        cost_estimate=pl.CostEstimate(flops=0, bytes_accessed=9 << 20, transcendentals=0),
        name="scale_common",
    )(common_geno)


def common_body(dest_ref, row_ref, *refs):
    panels, owned_ref = refs[:NY], refs[NY]
    outs = refs[NY + 1 : NY + 2 + NZ]
    joined, turned = refs[NY + 2 + NZ :]
    step = pl.program_id(0)
    sites = joined.shape[0] // N_COL

    @pl.when(step == 0)
    def _():
        for dy in range(NY):
            for dx in range(NX):
                start = pl.multiple_of(row_ref[dy * NX + dx], sites)
                joined[pl.ds(start, sites), :] = panels[dy][dx * sites : (dx + 1) * sites, :]
        turned[...] = joined[...].T

    part = jnp.dot(turned[...], owned_ref[...], preferred_element_type=F32)
    for q in range(N_SITE):

        @pl.when(step == q)
        def _():
            if q < NZ:
                outs[NZ][q] = part
            else:
                outs[q - NZ][...] = part


def common_product(received, dests, rows, panels):
    sites = received.shape[0] * received.shape[1]
    flat = received.reshape(sites, received.shape[2])
    return pl.pallas_call(
        common_body,
        grid_spec=pltpu.PrefetchScalarGridSpec(
            num_scalar_prefetch=2,
            grid=(N_SITE,),
            in_specs=[spec(panels[0].shape, lambda q, dest, row: (0, 0))] * NY
            + [spec((sites, TILE), lambda q, dest, row: (0, dest[q]))],
            out_specs=[spec((PANEL, TILE), lambda q, dest, row: (0, 0))] * NZ
            + [spec((NZ, PANEL, TILE), lambda q, dest, row: (0, 0, 0))],
            scratch_shapes=[pltpu.VMEM((sites, PANEL), BF), pltpu.VMEM((PANEL, sites), BF)],
        ),
        out_shape=[jax.ShapeDtypeStruct((PANEL, TILE), F32)] * NZ
        + [jax.ShapeDtypeStruct((NZ, PANEL, TILE), F32)],
        compiler_params=pltpu.CompilerParams(vmem_limit_bytes=VLIM),
        cost_estimate=pl.CostEstimate(
            flops=2 * sites * PANEL * TILE * N_SITE, bytes_accessed=9 << 20, transcendentals=0
        ),
        name="common_product",
    )(dests, rows, *panels, flat)


HALF = 64
EARLY = 5


def accumulate(place_ref, slices, panels, acc, made, first):
    for q in range(len(slices)):
        made[...] = jnp.dot(slices[q][...], panels[q][:SBLK, :], preferred_element_type=F32)
        for k in range(BLKS):
            at = place_ref[(first + q) * BLKS + k]
            acc[at] = acc[at] + made[k * SLICE : (k + 1) * SLICE, :]


def early_body(place_ref, *refs):
    slices, panels = refs[:EARLY], refs[EARLY : 2 * EARLY]
    acc, made = refs[2 * EARLY :]
    acc[...] = jnp.zeros_like(acc)
    accumulate(place_ref, slices, panels, acc, made, 0)


def late_body(place_ref, acc_in, *refs):
    late = N_SITE - EARLY
    slices, panels = refs[:late], refs[late : 2 * late]
    acc = refs[2 * late]
    outs = refs[2 * late + 1 : 2 * late + 11]
    made, sem = refs[2 * late + 11 :]
    accumulate(place_ref, slices, panels, acc, made, EARLY)
    copies = []
    for h in range(2):
        base = h * HALF
        up, down, keep1, keep3, own = outs[5 * h : 5 * h + 5]

        def unit(u, lo, hi):
            return acc.at[base + u * 16 + lo : base + u * 16 + hi]

        copies += [
            (unit(2, 0, 8), up.at[0:8]),
            (unit(1, 8, 16), up.at[8:16]),
            (unit(2, 8, 16), down.at[0:8]),
            (unit(3, 0, 8), down.at[8:16]),
            (unit(1, 0, 8), keep1),
            (unit(3, 8, 16), keep3),
            (unit(0, 0, 16), own),
        ]
    started = [
        pltpu.make_async_copy(src, dst, sem.at[i]) for i, (src, dst) in enumerate(copies)
    ]
    for one in started:
        one.start()
    for one in started:
        one.wait()


def rare_cost(sources):
    return pl.CostEstimate(
        flops=2 * sources * BLKS * SLICE * SBLK * PANEL, bytes_accessed=sources << 20, transcendentals=0
    )


def rare_product(places, slices, panels):
    dense = (2 * HALF, SLICE, PANEL)
    smem = pl.BlockSpec(memory_space=pltpu.SMEM)
    acc = pl.pallas_call(
        early_body,
        in_specs=[smem] + [whole_vmem()] * (2 * EARLY),
        out_specs=whole_vmem(),
        out_shape=pltpu.VMEM(dense, F32),
        scratch_shapes=[pltpu.VMEM((BLKS * SLICE, PANEL), F32)],
        compiler_params=pltpu.CompilerParams(vmem_limit_bytes=24 << 20),
        cost_estimate=rare_cost(EARLY),
        name="rare_early",
    )(places, *slices[:EARLY], *panels[:EARLY])
    late = N_SITE - EARLY
    half = [pltpu.HBM((n, SLICE, PANEL), F32) for n in (16, 16, 8, 8, 16)]
    half_specs = [pl.BlockSpec(memory_space=pltpu.HBM)] * 5
    return pl.pallas_call(
        late_body,
        in_specs=[smem, whole_vmem()] + [whole_vmem()] * (2 * late),
        out_specs=[whole_vmem()] + half_specs * 2,
        out_shape=[pltpu.VMEM(dense, F32)] + half * 2,
        scratch_shapes=[
            pltpu.VMEM((BLKS * SLICE, PANEL), F32),
            pltpu.SemaphoreType.DMA((14,)),
        ],
        input_output_aliases={1: 0},
        compiler_params=pltpu.CompilerParams(vmem_limit_bytes=24 << 20),
        cost_estimate=rare_cost(late),
        name="rare_late",
    )(places, acc, *slices[EARLY:], *panels[EARLY:])[1:]


def sum_body(mine, swapped, a, b, c, out_ref):
    out_ref[...] = mine[...] + swapped[0] + a[...] + b[...] + c[...]


def sum_parts(parts):
    rows = PANEL // 4
    block = spec((rows, TILE), lambda i: (i, 0))
    return pl.pallas_call(
        sum_body,
        grid=(4,),
        in_specs=[block, spec((1, rows, TILE), lambda i: (0, i, 0)), block, block, block],
        out_specs=block,
        out_shape=jax.ShapeDtypeStruct((PANEL, TILE), F32),
        compiler_params=pltpu.CompilerParams(vmem_limit_bytes=16 << 20),
        cost_estimate=pl.CostEstimate(flops=0, bytes_accessed=3 << 20, transcendentals=0),
        name="sum_parts",
    )(*parts)


def finish_body(row_ref, common_ref, *refs):
    pieces, out_ref, turned = refs[:N_SITE], refs[N_SITE], refs[N_SITE + 1]
    for q in range(N_SITE):
        start = pl.multiple_of(row_ref[q], SLICE)
        turned[pl.ds(start, SLICE), :] = pieces[q][...]
    out_ref[...] = (common_ref[...] + turned[...].T) * (1.0 / 8192)


def finish(rows, common, pieces):
    return pl.pallas_call(
        finish_body,
        in_specs=[pl.BlockSpec(memory_space=pltpu.SMEM)] + [whole_vmem()] * (1 + N_SITE),
        out_specs=whole_vmem(),
        out_shape=jax.ShapeDtypeStruct((PANEL, TILE), F32),
        scratch_shapes=[pltpu.VMEM((TILE, PANEL), F32)],
        compiler_params=pltpu.CompilerParams(vmem_limit_bytes=16 << 20),
        cost_estimate=pl.CostEstimate(flops=0, bytes_accessed=2 << 20, transcendentals=0),
        name="finish",
    )(rows, common, *pieces)


def along_site(dz, flip):
    return [
        (z * 2 + core, (z + dz) % NZ * 2 + (core ^ flip)) for z in range(NZ) for core in range(2)
    ]


def along_x(step):
    return [(x * NY + y, (x + step) % NX * NY + y) for x in range(NX) for y in range(NY)]


def along_y(step):
    return [(x * NY + y, x * NY + (y + step) % NY) for x in range(NX) for y in range(NY)]


def ring_open(up, down, perm):
    return lax.ppermute(up, "col", perm(1)), lax.ppermute(down, "col", perm(-1))


PIECES = (8, SLICE, PANEL)


def piece(n, shift):
    return spec((n, SLICE, PANEL), lambda i: (i + shift, 0, 0))


def add_body(*refs):
    for h in range(4):
        refs[8 + h][...] = refs[2 * h][...] + refs[2 * h + 1][...]


def close_sums(open_a, open_b, keeps):
    args = []
    for arrived, keep in zip((*open_a, *open_b), keeps):
        args += [arrived, keep]
    return pl.pallas_call(
        add_body,
        grid=(2,),
        in_specs=[piece(4, 0)] * 8,
        out_specs=[piece(4, 0)] * 4,
        out_shape=[jax.ShapeDtypeStruct(PIECES, F32)] * 4,
        compiler_params=pltpu.CompilerParams(vmem_limit_bytes=VLIM),
        cost_estimate=pl.CostEstimate(flops=0, bytes_accessed=6 << 20, transcendentals=0),
        name="close_sums",
    )(*args)


def pre_sums(open_a, open_b, own_a, own_b):
    args, maps = [], []
    for (low, high), own in ((open_a, own_a), (open_b, own_b)):
        args += [own, high, own, low]
        maps += [piece(4, 0), piece(4, 2), piece(4, 2), piece(4, 2)]
    return pl.pallas_call(
        add_body,
        grid=(2,),
        in_specs=maps,
        out_specs=[piece(4, 0)] * 4,
        out_shape=[jax.ShapeDtypeStruct(PIECES, F32)] * 4,
        compiler_params=pltpu.CompilerParams(vmem_limit_bytes=VLIM),
        cost_estimate=pl.CostEstimate(flops=0, bytes_accessed=6 << 20, transcendentals=0),
        name="pre_sums",
    )(*args)


def line_body(*refs):
    step = pl.program_id(0)
    for h in range(4):
        total = refs[2 * h][...] + refs[2 * h + 1][...]
        for part in range(2):

            @pl.when(step == part)
            def _():
                refs[8 + 2 * h + part][...] = total


def line_sums(pre, closed):
    args = []
    for one, two in zip(pre, closed):
        args += [one, two]
    return pl.pallas_call(
        line_body,
        grid=(2,),
        in_specs=[piece(4, 0)] * 8,
        out_specs=[spec((4, SLICE, PANEL), lambda i: (0, 0, 0))] * 8,
        out_shape=[jax.ShapeDtypeStruct((4, SLICE, PANEL), F32)] * 8,
        compiler_params=pltpu.CompilerParams(vmem_limit_bytes=VLIM),
        cost_estimate=pl.CostEstimate(flops=0, bytes_accessed=6 << 20, transcendentals=0),
        name="line_sums",
    )(*args)


def direct(own, one, two, three, perm):
    far = lax.ppermute(two, "col", perm(2))
    low = lax.ppermute(one, "col", perm(1))
    high = lax.ppermute(three, "col", perm(-1))
    return [own, low, high, far]


def join_body(dest_ref, *refs):
    parts, outs, whole = refs[:8], refs[8 : 8 + N_SITE], refs[8 + N_SITE]
    for h in range(2):
        own, low, high, far = parts[4 * h : 4 * h + 4]
        whole[4 * h : 4 * h + 4] = own[...] + low[...] + high[...] + far[...]
    for q in range(N_SITE):
        outs[q][...] = whole[dest_ref[q]]


def join(dests, a, b):
    return pl.pallas_call(
        join_body,
        in_specs=[pl.BlockSpec(memory_space=pltpu.SMEM)] + [whole_vmem()] * 8,
        out_specs=[whole_vmem()] * N_SITE,
        out_shape=[jax.ShapeDtypeStruct((SLICE, PANEL), F32)] * N_SITE,
        scratch_shapes=[pltpu.VMEM((N_SITE, SLICE, PANEL), F32)],
        compiler_params=pltpu.CompilerParams(vmem_limit_bytes=16 << 20),
        cost_estimate=pl.CostEstimate(flops=0, bytes_accessed=5 << 19, transcendentals=0),
        name="join",
    )(dests, *a, *b)


def per_device(common_geno, rare_values, block_tile, panel_rare):
    site = lax.axis_index("site")
    col = lax.axis_index("col")
    z, core = site // 2, site % 2
    x, y = col // NY, col % NY
    order = [(dz, flip) for dz in range(NZ) for flip in range(2)]
    dests_of = {(dz, flip): (z + dz) % NZ * 2 + (core ^ flip) for dz, flip in order}
    sources_of = {(dz, flip): (z - dz) % NZ * 2 + (core ^ flip) for dz, flip in order}
    dests = jnp.stack([dests_of[one] for one in order]).astype(jnp.int32)

    tile_row = jnp.zeros((16, PANEL), BF).at[0, :BLKS].set(block_tile.astype(BF))
    panel_plus = jnp.concatenate([panel_rare, tile_row], axis=0)
    near = [panel_plus] + [
        lax.ppermute(panel_plus, "site", along_site(dz, 0)) for dz in range(1, NZ)
    ]

    scaled, panel_part = scale(common_geno)
    line = [panel_part] + [lax.ppermute(panel_part, "col", along_x(d)) for d in (1, 2, 3)]
    scaled, offsets = lax.optimization_barrier((scaled, dests * SLICE))
    received = lax.all_to_all(scaled, "col", split_axis=0, concat_axis=0, tiled=True)

    packed = pack(rare_values, offsets)
    far = [lax.ppermute(one, "site", along_site(0, 1)) for one in near]
    panels = [(near, far)[flip][dz] for dz, flip in order]
    slices = [packed[0]]
    for q in range(1, N_SITE):
        slices.append(lax.ppermute(packed[q], "site", along_site(*order[q])))

    tiles = jnp.stack([one[SBLK, :BLKS] for one in panels]).astype(jnp.int32).reshape(-1)
    tile_site, tile_col = tiles // N_COL, tiles % N_COL
    u = (tile_col // NY - x) % NX
    v = (tile_col % NY - y) % NY
    places = jnp.where(tile_site < 4, u * 16 + v * 4, HALF + v * 16 + u * 4) + tile_site % 4
    ring_parts = rare_product(places.astype(jnp.int32), slices, panels)

    line = jnp.concatenate(line, axis=0)
    plane = [line] + [lax.ppermute(line, "col", along_y(d)) for d in (1, 2, 3)]
    sites = panel_part.shape[0]
    rows = [((x - dx) % NX * NY + (y - dy) % NY) * sites for dy in range(NY) for dx in range(NX)]
    rows = jnp.stack(rows).astype(jnp.int32)

    half_dests = [dests_of[dz, flip] for flip in (1, 0) for dz in range(NZ)]
    half_dests = jnp.stack(half_dests).astype(jnp.int32)
    ring_parts, half_dests = lax.optimization_barrier((ring_parts, half_dests))
    *mine, theirs = common_product(received, half_dests, rows, plane)
    swapped = lax.ppermute(theirs, "site", along_site(0, 1))

    open_a = ring_open(*ring_parts[:2], along_x)
    open_b = ring_open(*ring_parts[5:7], along_y)
    common = [lax.ppermute(mine[dz] + swapped[dz], "site", along_site(dz, 0)) for dz in (2, 1, 3)]
    common = [mine[0], swapped] + common
    keeps = (*ring_parts[2:4], *ring_parts[7:9])
    sent = close_sums(open_a, open_b, keeps)
    closed = [
        lax.ppermute(one, "col", perm(step))
        for one, perm, step in zip(sent, (along_x, along_x, along_y, along_y), (1, -1, 1, -1))
    ]
    pre = pre_sums(open_a, open_b, ring_parts[4], ring_parts[9])
    lines = line_sums(pre, closed)
    a = direct(*lines[:4], along_y)
    b = direct(*lines[4:], along_x)
    pieces = join(dests, a, b)
    moved = {q: lax.ppermute(pieces[q], "site", along_site(*order[q])) for q in (4, 5, 2, 3, 6, 7, 1)}
    moved[0] = pieces[0]
    sources = jnp.stack([sources_of[one] * SLICE for one in order]).astype(jnp.int32)
    return finish(sources, sum_parts(common), [moved[q] for q in range(N_SITE)])


def solution(mesh):
    placed = (
        P(("site", "col"), None),
        P(("site", "col"), None, None),
        P(("site", "col")),
        P(("site", "col"), None),
    )
    return jax.shard_map(
        per_device, mesh=mesh, in_specs=placed, out_specs=P(None, ("site", "col")), check_vma=False
    )
```

time: 276 us -> 267 us (0.967)
  starting transfers between devices: 79.1 us -> 62.2 us
  local copies, waits for them, and re-layouts: 5.91 us -> 21.5 us
  other arithmetic: 5.26 us -> 0.88 us
    ppermute x24 -> x34, waiting for transfers between devices: 103 us -> 122 us  [the longest x3 52.4 us: per_device(): lax.ppermute(panel_part, 'col', along_x(d))]
    ppermute x24 -> x34, starting transfers between devices: 55.6 us -> 40 us  [the longest x7 11.6 us: per_device(): lax.ppermute(pieces[q], 'site', along_site(*order[q]))]
    unnamed x49 -> x71, local copies, waits for them, and re-layouts: 4.25 us -> 18.8 us
    ppermute x2, waiting for transfers between devices: 34.4 us -> 21.6 us  [ring_open(): lax.ppermute(down, 'col', perm(-1))]
    ppermute x3, waiting for transfers between devices: 8.22 us -> 0.01 us  [per_device(): lax.ppermute(panel_plus, 'site', along_site(dz, 0))]
    all_to_all x1 -> x0, starting transfers between devices: 3.44 us -> none  [per_device(): lax.all_to_all(reduced, 'site', split_axis=0, concat_axis=0, tiled=True)]
    ppermute x2, starting transfers between devices: 5.28 us -> 2.32 us  [ring_open(): lax.ppermute(down, 'col', perm(-1))]
    pallas_call x3 -> x8, Pallas kernels: 13 us -> 13.4 us  [the longest x1 5.82 us: rare_product(): pl.pallas_call(late_body, in_specs=[smem, whole_vmem()] + [whole_vmem()]...]
  transfers between devices with their start and end apart: 37 -> 46, of which waited for: 19 -> 21; matrix products, arithmetic and copies ran while one was open for 2% -> 2% of each run, Pallas kernels for 9% -> 7%
where the time goes in v2:
time: 267 us; the launch traced here: 266 us
  waiting for transfers between devices  146 us (55%)
  starting transfers between devices  62.2 us (23%)
  Pallas kernels  34.9 us (13%)
  local copies, waits for them, and re-layouts  21.5 us (8%)
    ppermute x3, waiting for transfers between devices, per_device(): lax.ppermute(panel_part, 'col', along_x(d))  52.4 us
    ppermute x7, waiting for transfers between devices, per_device(): slices.append(lax.ppermute(packed[q], 'site', along_site(*order[q])))  42.2 us
    ppermute x2, waiting for transfers between devices, ring_open(): lax.ppermute(down, 'col', perm(-1))  21.6 us
    unnamed x71, local copies, waits for them, and re-layouts  18.8 us
    ppermute x7, starting transfers between devices, per_device(): lax.ppermute(pieces[q], 'site', along_site(*order[q]))  11.6 us
    ppermute x7, starting transfers between devices, per_device(): slices.append(lax.ppermute(packed[q], 'site', along_site(*order[q])))  10.3 us
    ppermute x4, waiting for transfers between devices, per_device(): lax.ppermute(one, 'col', perm(step))  9.75 us
    pallas_call x1, Pallas kernels, common_product(): pl.pallas_call(common_body, grid_spec=pltpu.PrefetchScalarGridSpec(num_sc...  8.11 us
  transfers between devices with their start and end apart: 46, of which 21 were waited for; matrix products, arithmetic and copies ran while one was open for 2% of the time, Pallas kernels for 7%

profile of v2, /device:TPU:1, one launch (start us, length us, event | category | flops | bytes accessed | tf_op | source)
XLA Modules:
  0.0 265.6 jit_solution(320348054846530585)
XLA Ops:
  0.0 5.6 %scale_common.1 = (bf16[16,64,2048]{2,1,0:T(8,128)(2,1)}, bf16[64,512]{1,0:T(8,128)(2,1)}) custom-call(bf16[64,32768]{1,0:T(8,128)(2,1)} %x_ref.2), custom_call_target="tpu_custom_call" | custom-call | bytes 9437184 | tf_op jit(solution)/shard_map/scale_common/pallas_call | solution.py:82
  6.3 7.8 %all-to-all-start = ((bf16[16,64,2048]{2,1,0:T(8,128)(2,1)}), bf16[16,64,2048]{2,1,0:T(8,128)(2,1)}, u32[]{:S(2)}, u32[]{:S(2)}) async-start(bf16[16,64,2048]{2,1,0:T(8,128)(2,1)} %get-tuple-element.101), calls=%async_computation | async-start | bytes 8388608 | tf_op jit(solution)/shard_map/all_to_all | solution.py:418
  14.2 1.7 collective-permute-start.1
  15.9 7.8 %pack_rare.1 = (bf16[512,512]{1,0:T(8,128)(2,1)}, bf16[512,512]{1,0:T(8,128)(2,1)}, bf16[512,512]{1,0:T(8,128)(2,1)}, bf16[512,512]{1,0:T(8,128)(2,1)}, bf16[512...) custom-call(s32[8]{0:T(128)} %broadcast_multiply_fusion.off_ref, ...), custom_call_target="tpu_custom_call" | custom-call | bytes 8388608 | tf_op jit(solution)/shard_map/pack_rare/pallas_call | solution.py:45
  23.7 1.3 collective-permute-start.7
  25.0 3.3 %collective-permute-start.3 = (bf16[528,512]{1,0:T(8,128)(2,1)S(1)}, bf16[528,512]{1,0:T(8,128)(2,1)S(1)}, u32[]{:S(2)}, u32[]{:S(2)}) collective-permute-start(bf16[528,512]{1,0:T(8,128)(2,1)S(1)} %fusion.1.refs_5_), channel_id=1, source_target_pairs={{0,64},{16,80},{32,96},{48,112},{64,0},{80,16},{96,32},{112,48},{1... | collective-permute-start | bytes 1622024 | tf_op jit(solution)/shard_map/ppermute | solution.py:412
  29.0 1.6 collective-permute-start.14
  30.6 45.1 %collective-permute-done.14 = bf16[64,512]{1,0:T(8,128)(2,1)} collective-permute-done((bf16[64,512]{1,0:T(8,128)(2,1)S(1)}, bf16[64,512]{1,0:T(8,128)(2,1)}, u32[]{:S(2)}, u32[]{:S(2)}) %collective-permute-start.14) | collective-permute-done | bytes 65568 | tf_op jit(solution)/shard_map/ppermute | solution.py:416
  75.7 4.6 %collective-permute-done.15 = bf16[64,512]{1,0:T(8,128)(2,1)S(1)} collective-permute-done((bf16[64,512]{1,0:T(8,128)(2,1)S(1)}, bf16[64,512]{1,0:T(8,128)(2,1)S(1)}, u32[]{:S(2)}, u32[]{:S(2)}) %collective-permute-start.15) | collective-permute-done | bytes 65568 | tf_op jit(solution)/shard_map/ppermute | solution.py:416
  80.3 1.7 collective-permute-start.16
  82.0 2.7 %collective-permute-done.16 = bf16[64,512]{1,0:T(8,128)(2,1)S(1)} collective-permute-done((bf16[64,512]{1,0:T(8,128)(2,1)S(1)}, bf16[64,512]{1,0:T(8,128)(2,1)S(1)}, u32[]{:S(2)}, u32[]{:S(2)}) %collective-permute-start.16) | collective-permute-done | bytes 65568 | tf_op jit(solution)/shard_map/ppermute | solution.py:416
  84.7 4.2 %collective-permute-start = (bf16[528,512]{1,0:T(8,128)(2,1)S(1)}, bf16[528,512]{1,0:T(8,128)(2,1)S(1)}, u32[]{:S(2)}, u32[]{:S(2)}) collective-permute-start(bf16[528,512]{1,0:T(8,128)(2,1)S(1)} %fusion.1.refs_5_), channel_id=1, source_target_pairs={{0,16},{16,0},{32,48},{48,32},{64,80},{80,64},{96,112},{112,96},{1... | collective-permute-start | bytes 1622024 | tf_op jit(solution)/shard_map/ppermute | solution.py:421
  89.8 1.6 collective-permute-start.8
  92.2 13.4 %collective-permute-done.8.refs_2_ = bf16[512,512]{1,0:T(8,128)(2,1)S(1)} collective-permute-done((bf16[512,512]{1,0:T(8,128)(2,1)}, bf16[512,512]{1,0:T(8,128)(2,1)S(1)}, u32[]{:S(2)}, u32[]{:S(2)}) %collective-permute-start.8) | collective-permute-done | bytes 524320 | tf_op jit(solution)/shard_map/ppermute | solution.py:425
  106.7 3.3 %collective-permute-start.10 = (bf16[512,512]{1,0:T(8,128)(2,1)}, bf16[512,512]{1,0:T(8,128)(2,1)}, u32[]{:S(2)}, u32[]{:S(2)}) collective-permute-start(bf16[512,512]{1,0:T(8,128)(2,1)} %get-tuple-element.85), channel_id=1, source_target_pairs={{0,64},{16,80},{32,96},{48,112},{64,0},{80,16},{96,32},{112,48},{1... | collective-permute-start | bytes 1572872 | tf_op jit(solution)/shard_map/ppermute | solution.py:425
  113.5 2.0 collective-permute-start.12
  115.5 1.1 collective-permute-start.13
  119.8 2.9 %collective-permute-done.9.refs_3_ = bf16[512,512]{1,0:T(8,128)(2,1)} collective-permute-done((bf16[512,512]{1,0:T(8,128)(2,1)}, bf16[512,512]{1,0:T(8,128)(2,1)}, u32[]{:S(2)}, u32[]{:S(2)}) %collective-permute-start.9) | collective-permute-done | bytes 524320 | tf_op jit(solution)/shard_map/ppermute | solution.py:425
  122.7 11.1 %collective-permute-done.10.refs_4_ = bf16[512,512]{1,0:T(8,128)(2,1)} collective-permute-done((bf16[512,512]{1,0:T(8,128)(2,1)}, bf16[512,512]{1,0:T(8,128)(2,1)}, u32[]{:S(2)}, u32[]{:S(2)}) %collective-permute-start.10) | collective-permute-done | bytes 524320 | tf_op jit(solution)/shard_map/ppermute | solution.py:425
  133.8 10.3 %collective-permute-done.11.refs_0_ = bf16[512,512]{1,0:T(8,128)(2,1)} collective-permute-done((bf16[512,512]{1,0:T(8,128)(2,1)}, bf16[512,512]{1,0:T(8,128)(2,1)}, u32[]{:S(2)}, u32[]{:S(2)}) %collective-permute-start.11) | collective-permute-done | bytes 524320 | tf_op jit(solution)/shard_map/ppermute | solution.py:425
  144.1 1.0 copy-done.3
  145.2 1.0 copy-done.5
  149.3 3.2 %rare_early.1.acc_in = f32[128,32,512]{2,1,0:T(8,128)S(1)} custom-call(s32[128]{0:T(128)S(1)} %fusion.5.place_ref, bf16[512,512]{1,0:T(8,128)(2,1)S(1)} %copy-done.14, bf16[512,512]{1,0:T(8,128)(2,1)S(1)} %copy-done.16, bf16[512,512]{1,0:T(8,128)(2,1)S(1)} %copy-done.18, bf16[512,512]{1,0:T(8,128)(2,1)} %collective-permute-done.9.refs_3_, ...), custom_call_target="tpu_custom_call" | custom-call | flops 1342177280 | bytes 5242880 | tf_op jit(solution)/shard_map/rare_early/pallas_call | solution.py:211
  152.5 4.5 %collective-permute-done.13.refs_2_ = bf16[512,512]{1,0:T(8,128)(2,1)} collective-permute-done((bf16[512,512]{1,0:T(8,128)(2,1)}, bf16[512,512]{1,0:T(8,128)(2,1)}, u32[]{:S(2)}, u32[]{:S(2)}) %collective-permute-start.13) | collective-permute-done | bytes 524320 | tf_op jit(solution)/shard_map/ppermute | solution.py:425
  157.0 5.8 %rare_late.1 = (f32[128,32,512]{2,1,0:T(8,128)S(1)}, f32[16,32,512]{2,1,0:T(8,128)}, f32[16,32,512]{2,1,0:T(8,128)}, f32[8,32,512]{2,1,0:T(8,128)}, f32[8,32,512...) custom-call(s32[128]{0:T(128)S(1)} %fusion.5.place_ref, ...), custom_call_target="tpu_custom_call", output_to_operand_aliasing={{0}: (1, {})} | custom-call | flops 805306368 | bytes 3145728 | tf_op jit(solution)/shard_map/rare_late/pallas_call | solution.py:224
  167.9 8.1 %common_product.1 = (f32[512,256]{1,0:T(8,128)S(1)}, f32[512,256]{1,0:T(8,128)S(1)}, f32[512,256]{1,0:T(8,128)S(1)}, f32[512,256]{1,0:T(8,128)S(1)}, f32[4,512,256]{2,1,0:T(8,128)S(1)}) custom-call(s32[8]{0:T(128)S(1)} %stack.138.dest_ref, s32[16]{0:T(128)S(1)} %stack.155.row_ref, bf16[256,512]{1,0:T(8,128)(2,1)S(1)} %constant_dynamic-update-slice_fusion.refs_0_, ...), custom_call_target="tpu_custom_call" | custom-call | flops 2147483648 | bytes 9437184 | tf_op jit(solution)/shard_map/common_product/pallas_call | solution.py:129
  176.7 2.1 collective-permute-start.24
  179.1 1.3 collective-permute-start.27
  180.3 21.5 %collective-permute-done.24.refs_1_.refs_2_ = f32[16,32,512]{2,1,0:T(8,128)S(1)} collective-permute-done((f32[16,32,512]{2,1,0:T(8,128)S(1)}, f32[16,32,512]{2,1,0:T(8,128)S(1)}, u32[]{:S(2)}, u32[]{:S(2)}) %collective-permute-start.24) | collective-permute-done | bytes 1048608 | tf_op jit(solution)/shard_map/ppermute | solution.py:295
  201.9 2.5 collective-permute-done.25.refs_3_.refs_0_
  205.5 2.0 collective-permute-start.29
  207.6 2.5 collective-permute-start.31
  210.3 7.6 %collective-permute-done.28.refs_1_ = f32[8,32,512]{2,1,0:T(8,128)S(1)} collective-permute-done((f32[8,32,512]{2,1,0:T(8,128)S(1)}, f32[8,32,512]{2,1,0:T(8,128)S(1)}, u32[]{:S(2)}, u32[]{:S(2)}) %collective-permute-start.28) | collective-permute-done | bytes 524320 | tf_op jit(solution)/shard_map/ppermute | solution.py:453
  218.0 2.1 collective-permute-done.30.refs_5_
  221.2 2.0 collective-permute-start.33
  224.3 1.5 collective-permute-start.21
  225.8 1.2 collective-permute-done.32.refs_1_
  228.6 2.5 collective-permute-start.23
  231.1 1.8 collective-permute-done.34.refs_3_
  233.4 5.1 %collective-permute-done.36.refs_6_ = f32[4,32,512]{2,1,0:T(8,128)S(1)} collective-permute-done((f32[4,32,512]{2,1,0:T(8,128)S(1)}, f32[4,32,512]{2,1,0:T(8,128)S(1)}, u32[]{:S(2)}, u32[]{:S(2)}) %collective-permute-start.36) | collective-permute-done | bytes 262176 | tf_op jit(solution)/shard_map/ppermute | solution.py:373
  238.5 1.7 collective-permute-done.37.refs_7_
  240.2 1.4 join.1
  241.6 7.0 %collective-permute-start.38 = (f32[32,512]{1,0:T(8,128)S(1)}, f32[32,512]{1,0:T(8,128)S(1)}, u32[]{:S(2)}, u32[]{:S(2)}) collective-permute-start(f32[32,512]{1,0:T(8,128)S(1)} %get-tuple-element.134), channel_id=1, source_target_pairs={{0,16},{16,0},{32,48},{48,32},{64,80},{80,64},{96,112},{112,96},{1... | collective-permute-start | bytes 196616 | tf_op jit(solution)/shard_map/ppermute | solution.py:461
  249.5 4.0 %collective-permute-done.39.refs_2_ = f32[32,512]{1,0:T(8,128)S(1)} collective-permute-done((f32[32,512]{1,0:T(8,128)S(1)}, f32[32,512]{1,0:T(8,128)S(1)}, u32[]{:S(2)}, u32[]{:S(2)}) %collective-permute-start.39) | collective-permute-done | bytes 65568 | tf_op jit(solution)/shard_map/ppermute | solution.py:461
  253.5 4.0 %collective-permute-start.42 = (f32[32,512]{1,0:T(8,128)}, f32[32,512]{1,0:T(8,128)S(1)}, u32[]{:S(2)}, u32[]{:S(2)}) collective-permute-start(f32[32,512]{1,0:T(8,128)} %get-tuple-element.138), channel_id=1, source_target_pairs={{0,80},{16,64},{32,112},{48,96},{64,16},{80,0},{96,48},{112,32},{1... | collective-permute-start | bytes 196616 | tf_op jit(solution)/shard_map/ppermute | solution.py:461
  259.8 1.0 copy-done.7
  262.3 1.3 collective-permute-done.44.refs_7_
  263.6 1.9 finish.1
  (146 shorter events, 30.2 us)
Async XLA Ops:
  6.3 158.7 %all-to-all-start = ((bf16[16,64,2048]{2,1,0:T(8,128)(2,1)}), bf16[16,64,2048]{2,1,0:T(8,128)(2,1)}, u32[]{:S(2)}, u32[]{:S(2)}) async-start(bf16[16,64,2048]{2,1,0:T(8,128)(2,1)} %get-tuple-element.101), calls=%async_computation | async-start | bytes 8388608 | tf_op jit(solution)/shard_map/all_to_all | solution.py:418
  14.2 74.7 %collective-permute-start.1 = (bf16[528,512]{1,0:T(8,128)(2,1)S(1)}, bf16[528,512]{1,0:T(8,128)(2,1)S(1)}, u32[]{:S(2)}, u32[]{:S(2)}) collective-permute-start(bf16[528,512]{1,0:T(8,128)(2,1)S(1)} %fusion.1.refs_5_), channel_id=1, source_target_pairs={{0,32},{16,48},{32,64},{48,80},{64,96},{80,112},{96,0},{112,16},{1... | collective-permute-start | bytes 1622024 | tf_op jit(solution)/shard_map/ppermute | solution.py:412
  23.7 65.3 %collective-permute-start.7 = (bf16[512,512]{1,0:T(8,128)(2,1)}, bf16[512,512]{1,0:T(8,128)(2,1)S(1)}, u32[]{:S(2)}, u32[]{:S(2)}) collective-permute-start(bf16[512,512]{1,0:T(8,128)(2,1)} %get-tuple-element.82), channel_id=1, source_target_pairs={{0,16},{16,0},{32,48},{48,32},{64,80},{80,64},{96,112},{112,96},{1... | collective-permute-start | bytes 1572872 | tf_op jit(solution)/shard_map/ppermute | solution.py:425
  25.0 66.4 %collective-permute-start.3 = (bf16[528,512]{1,0:T(8,128)(2,1)S(1)}, bf16[528,512]{1,0:T(8,128)(2,1)S(1)}, u32[]{:S(2)}, u32[]{:S(2)}) collective-permute-start(bf16[528,512]{1,0:T(8,128)(2,1)S(1)} %fusion.1.refs_5_), channel_id=1, source_target_pairs={{0,64},{16,80},{32,96},{48,112},{64,0},{80,16},{96,32},{112,48},{1... | collective-permute-start | bytes 1622024 | tf_op jit(solution)/shard_map/ppermute | solution.py:412
  28.3 63.8 %collective-permute-start.5 = (bf16[528,512]{1,0:T(8,128)(2,1)S(1)}, bf16[528,512]{1,0:T(8,128)(2,1)S(1)}, u32[]{:S(2)}, u32[]{:S(2)}) collective-permute-start(bf16[528,512]{1,0:T(8,128)(2,1)S(1)} %fusion.1.refs_5_), channel_id=1, source_target_pairs={{0,96},{16,112},{32,0},{48,16},{64,32},{80,48},{96,64},{112,80},{1... | collective-permute-start | bytes 1622024 | tf_op jit(solution)/shard_map/ppermute | solution.py:412
  29.0 46.7 %collective-permute-start.14 = (bf16[64,512]{1,0:T(8,128)(2,1)S(1)}, bf16[64,512]{1,0:T(8,128)(2,1)}, u32[]{:S(2)}, u32[]{:S(2)}) collective-permute-start(bf16[64,512]{1,0:T(8,128)(2,1)S(1)} %copy-done.26), channel_id=1, source_target_pairs={{0,4},{1,5},{2,6},{3,7},{4,8},{5,9},{6,10},{7,11},{8,12},{9,13},{1... | collective-permute-start | bytes 196616 | tf_op jit(solution)/shard_map/ppermute | solution.py:416
  75.7 4.6 %collective-permute-start.15 = (bf16[64,512]{1,0:T(8,128)(2,1)S(1)}, bf16[64,512]{1,0:T(8,128)(2,1)S(1)}, u32[]{:S(2)}, u32[]{:S(2)}) collective-permute-start(bf16[64,512]{1,0:T(8,128)(2,1)S(1)} %copy-done.26), channel_id=1, source_target_pairs={{0,8},{1,9},{2,10},{3,11},{4,12},{5,13},{6,14},{7,15},{8,0},{9,1},... | collective-permute-start | bytes 196616 | tf_op jit(solution)/shard_map/ppermute | solution.py:416
  80.3 4.4 %collective-permute-start.16 = (bf16[64,512]{1,0:T(8,128)(2,1)S(1)}, bf16[64,512]{1,0:T(8,128)(2,1)S(1)}, u32[]{:S(2)}, u32[]{:S(2)}) collective-permute-start(bf16[64,512]{1,0:T(8,128)(2,1)S(1)} %copy-done.26), channel_id=1, source_target_pairs={{0,12},{1,13},{2,14},{3,15},{4,0},{5,1},{6,2},{7,3},{8,4},{9,5},{1... | collective-permute-start | bytes 196616 | tf_op jit(solution)/shard_map/ppermute | solution.py:416
  84.7 21.9 %collective-permute-start = (bf16[528,512]{1,0:T(8,128)(2,1)S(1)}, bf16[528,512]{1,0:T(8,128)(2,1)S(1)}, u32[]{:S(2)}, u32[]{:S(2)}) collective-permute-start(bf16[528,512]{1,0:T(8,128)(2,1)S(1)} %fusion.1.refs_5_), channel_id=1, source_target_pairs={{0,16},{16,0},{32,48},{48,32},{64,80},{80,64},{96,112},{112,96},{1... | collective-permute-start | bytes 1622024 | tf_op jit(solution)/shard_map/ppermute | solution.py:421
  88.9 21.1 %collective-permute-start.2 = (bf16[528,512]{1,0:T(8,128)(2,1)S(1)}, bf16[528,512]{1,0:T(8,128)(2,1)S(1)}, u32[]{:S(2)}, u32[]{:S(2)}) collective-permute-start(bf16[528,512]{1,0:T(8,128)(2,1)S(1)} %collective-permute-done.1.refs_7_), channel_id=1, source_target_pairs={{0,16},{16,0},{32,48},{48,32},{64,80},{80,64},{96,112},{112,96},{1... | collective-permute-start | bytes 1622024 | tf_op jit(solution)/shard_map/ppermute | solution.py:421
  89.8 15.8 %collective-permute-start.8 = (bf16[512,512]{1,0:T(8,128)(2,1)}, bf16[512,512]{1,0:T(8,128)(2,1)S(1)}, u32[]{:S(2)}, u32[]{:S(2)}) collective-permute-start(bf16[512,512]{1,0:T(8,128)(2,1)} %get-tuple-element.83), channel_id=1, source_target_pairs={{0,32},{16,48},{32,64},{48,80},{64,96},{80,112},{96,0},{112,16},{1... | collective-permute-start | bytes 1572872 | tf_op jit(solution)/shard_map/ppermute | solution.py:425
  91.4 22.1 %collective-permute-start.4 = (bf16[528,512]{1,0:T(8,128)(2,1)S(1)}, bf16[528,512]{1,0:T(8,128)(2,1)S(1)}, u32[]{:S(2)}, u32[]{:S(2)}) collective-permute-start(bf16[528,512]{1,0:T(8,128)(2,1)S(1)} %collective-permute-done.3.refs_9_), channel_id=1, source_target_pairs={{0,16},{16,0},{32,48},{48,32},{64,80},{80,64},{96,112},{112,96},{1... | collective-permute-start | bytes 1622024 | tf_op jit(solution)/shard_map/ppermute | solution.py:421
  92.1 23.3 %collective-permute-start.6 = (bf16[528,512]{1,0:T(8,128)(2,1)S(1)}, bf16[528,512]{1,0:T(8,128)(2,1)S(1)}, u32[]{:S(2)}, u32[]{:S(2)}) collective-permute-start(bf16[528,512]{1,0:T(8,128)(2,1)S(1)} %collective-permute-done.5.refs_4_), channel_id=1, source_target_pairs={{0,16},{16,0},{32,48},{48,32},{64,80},{80,64},{96,112},{112,96},{1... | collective-permute-start | bytes 1622024 | tf_op jit(solution)/shard_map/ppermute | solution.py:421
  106.4 16.3 %collective-permute-start.9 = (bf16[512,512]{1,0:T(8,128)(2,1)}, bf16[512,512]{1,0:T(8,128)(2,1)}, u32[]{:S(2)}, u32[]{:S(2)}) collective-permute-start(bf16[512,512]{1,0:T(8,128)(2,1)} %get-tuple-element.84), channel_id=1, source_target_pairs={{0,48},{16,32},{32,80},{48,64},{64,112},{80,96},{96,16},{112,0},{1... | collective-permute-start | bytes 1572872 | tf_op jit(solution)/shard_map/ppermute | solution.py:425
  106.7 27.1 %collective-permute-start.10 = (bf16[512,512]{1,0:T(8,128)(2,1)}, bf16[512,512]{1,0:T(8,128)(2,1)}, u32[]{:S(2)}, u32[]{:S(2)}) collective-permute-start(bf16[512,512]{1,0:T(8,128)(2,1)} %get-tuple-element.85), channel_id=1, source_target_pairs={{0,64},{16,80},{32,96},{48,112},{64,0},{80,16},{96,32},{112,48},{1... | collective-permute-start | bytes 1572872 | tf_op jit(solution)/shard_map/ppermute | solution.py:425
  110.8 33.3 %collective-permute-start.11 = (bf16[512,512]{1,0:T(8,128)(2,1)}, bf16[512,512]{1,0:T(8,128)(2,1)}, u32[]{:S(2)}, u32[]{:S(2)}) collective-permute-start(bf16[512,512]{1,0:T(8,128)(2,1)} %get-tuple-element.86), channel_id=1, source_target_pairs={{0,80},{16,64},{32,112},{48,96},{64,16},{80,0},{96,48},{112,32},{1... | collective-permute-start | bytes 1572872 | tf_op jit(solution)/shard_map/ppermute | solution.py:425
  113.5 39.1 %collective-permute-start.12 = (bf16[512,512]{1,0:T(8,128)(2,1)}, bf16[512,512]{1,0:T(8,128)(2,1)}, u32[]{:S(2)}, u32[]{:S(2)}) collective-permute-start(bf16[512,512]{1,0:T(8,128)(2,1)} %get-tuple-element.87), channel_id=1, source_target_pairs={{0,96},{16,112},{32,0},{48,16},{64,32},{80,48},{96,64},{112,80},{1... | collective-permute-start | bytes 1572872 | tf_op jit(solution)/shard_map/ppermute | solution.py:425
  115.5 41.6 %collective-permute-start.13 = (bf16[512,512]{1,0:T(8,128)(2,1)}, bf16[512,512]{1,0:T(8,128)(2,1)}, u32[]{:S(2)}, u32[]{:S(2)}) collective-permute-start(bf16[512,512]{1,0:T(8,128)(2,1)} %get-tuple-element.88), channel_id=1, source_target_pairs={{0,112},{16,96},{32,16},{48,0},{64,48},{80,32},{96,80},{112,64},{1... | collective-permute-start | bytes 1572872 | tf_op jit(solution)/shard_map/ppermute | solution.py:425
  122.7 40.1 %collective-permute-start.17 = (bf16[256,512]{1,0:T(8,128)(2,1)S(1)}, bf16[256,512]{1,0:T(8,128)(2,1)S(1)}, u32[]{:S(2)}, u32[]{:S(2)}) collective-permute-start(bf16[256,512]{1,0:T(8,128)(2,1)S(1)} %constant_dynamic-update-slice_fusion.refs_0_), channel_id=1, source_target_pairs={{0,1},{1,2},{2,3},{3,0},{4,5},{5,6},{6,7},{7,4},{8,9},{9,10},{10,1... | collective-permute-start | bytes 786440 | tf_op jit(solution)/shard_map/ppermute | solution.py:435
  133.8 29.8 %collective-permute-start.18 = (bf16[256,512]{1,0:T(8,128)(2,1)S(1)}, bf16[256,512]{1,0:T(8,128)(2,1)S(1)}, u32[]{:S(2)}, u32[]{:S(2)}) collective-permute-start(bf16[256,512]{1,0:T(8,128)(2,1)S(1)} %constant_dynamic-update-slice_fusion.refs_0_), channel_id=1, source_target_pairs={{0,2},{1,3},{2,0},{3,1},{4,6},{5,7},{6,4},{7,5},{8,10},{9,11},{10,... | collective-permute-start | bytes 786440 | tf_op jit(solution)/shard_map/ppermute | solution.py:435
  144.1 20.2 %collective-permute-start.19 = (bf16[256,512]{1,0:T(8,128)(2,1)S(1)}, bf16[256,512]{1,0:T(8,128)(2,1)S(1)}, u32[]{:S(2)}, u32[]{:S(2)}) collective-permute-start(bf16[256,512]{1,0:T(8,128)(2,1)S(1)} %constant_dynamic-update-slice_fusion.refs_0_), channel_id=1, source_target_pairs={{0,3},{1,0},{2,1},{3,2},{4,7},{5,4},{6,5},{7,6},{8,11},{9,8},{10,9... | collective-permute-start | bytes 786440 | tf_op jit(solution)/shard_map/ppermute | solution.py:435
  167.8 36.5 %copy-start.10 = (f32[8,32,512]{2,1,0:T(8,128)S(1)}, f32[8,32,512]{2,1,0:T(8,128)}, u32[]{:S(2)}) copy-start(f32[8,32,512]{2,1,0:T(8,128)} %get-tuple-element.114.refs_1_) | copy-start | bytes 1572868
  167.8 36.5 %copy-start.11 = (f32[8,32,512]{2,1,0:T(8,128)S(1)}, f32[8,32,512]{2,1,0:T(8,128)}, u32[]{:S(2)}) copy-start(f32[8,32,512]{2,1,0:T(8,128)} %get-tuple-element.115.refs_3_) | copy-start | bytes 1572868
  176.0 48.1 %collective-permute-start.20 = (f32[4,512,256]{2,1,0:T(8,128)S(1)}, f32[4,512,256]{2,1,0:T(8,128)S(1)}, u32[]{:S(2)}, u32[]{:S(2)}) collective-permute-start(f32[4,512,256]{2,1,0:T(8,128)S(1)} %get-tuple-element.103), channel_id=1, source_target_pairs={{0,16},{16,0},{32,48},{48,32},{64,80},{80,64},{96,112},{112,96},{1... | collective-permute-start | bytes 6291464 | tf_op jit(solution)/shard_map/ppermute | solution.py:444
  176.7 25.2 %collective-permute-start.24 = (f32[16,32,512]{2,1,0:T(8,128)S(1)}, f32[16,32,512]{2,1,0:T(8,128)S(1)}, u32[]{:S(2)}, u32[]{:S(2)}) collective-permute-start(f32[16,32,512]{2,1,0:T(8,128)S(1)} %copy-done.32), channel_id=1, source_target_pairs={{0,12},{1,13},{2,14},{3,15},{4,0},{5,1},{6,2},{7,3},{8,4},{9,5},{1... | collective-permute-start | bytes 3145736 | tf_op jit(solution)/shard_map/ppermute | solution.py:295
  178.8 25.6 %collective-permute-start.25 = (f32[16,32,512]{2,1,0:T(8,128)S(1)}, f32[16,32,512]{2,1,0:T(8,128)S(1)}, u32[]{:S(2)}, u32[]{:S(2)}) collective-permute-start(f32[16,32,512]{2,1,0:T(8,128)S(1)} %copy-done.31), channel_id=1, source_target_pairs={{0,4},{1,5},{2,6},{3,7},{4,8},{5,9},{6,10},{7,11},{8,12},{9,13},{1... | collective-permute-start | bytes 3145736 | tf_op jit(solution)/shard_map/ppermute | solution.py:295
  178.8 25.6 %collective-permute-start.26 = (f32[16,32,512]{2,1,0:T(8,128)S(1)}, f32[16,32,512]{2,1,0:T(8,128)S(1)}, u32[]{:S(2)}, u32[]{:S(2)}) collective-permute-start(f32[16,32,512]{2,1,0:T(8,128)S(1)} %copy-done.30), channel_id=1, source_target_pairs={{0,3},{1,0},{2,1},{3,2},{4,7},{5,4},{6,5},{7,6},{8,11},{9,8},{10,9... | collective-permute-start | bytes 3145736 | tf_op jit(solution)/shard_map/ppermute | solution.py:295
  179.1 25.3 %collective-permute-start.27 = (f32[16,32,512]{2,1,0:T(8,128)S(1)}, f32[16,32,512]{2,1,0:T(8,128)S(1)}, u32[]{:S(2)}, u32[]{:S(2)}) collective-permute-start(f32[16,32,512]{2,1,0:T(8,128)S(1)} %copy-done.29), channel_id=1, source_target_pairs={{0,1},{1,2},{2,3},{3,0},{4,5},{5,6},{6,7},{7,4},{8,9},{9,10},{10,1... | collective-permute-start | bytes 3145736 | tf_op jit(solution)/shard_map/ppermute | solution.py:295
  204.7 13.3 %collective-permute-start.28 = (f32[8,32,512]{2,1,0:T(8,128)S(1)}, f32[8,32,512]{2,1,0:T(8,128)S(1)}, u32[]{:S(2)}, u32[]{:S(2)}) collective-permute-start(f32[8,32,512]{2,1,0:T(8,128)S(1)} %get-tuple-element.118), channel_id=1, source_target_pairs={{0,4},{1,5},{2,6},{3,7},{4,8},{5,9},{6,10},{7,11},{8,12},{9,13},{1... | collective-permute-start | bytes 1572872 | tf_op jit(solution)/shard_map/ppermute | solution.py:453
  205.5 12.5 %collective-permute-start.29 = (f32[8,32,512]{2,1,0:T(8,128)S(1)}, f32[8,32,512]{2,1,0:T(8,128)S(1)}, u32[]{:S(2)}, u32[]{:S(2)}) collective-permute-start(f32[8,32,512]{2,1,0:T(8,128)S(1)} %get-tuple-element.120), channel_id=1, source_target_pairs={{0,12},{1,13},{2,14},{3,15},{4,0},{5,1},{6,2},{7,3},{8,4},{9,5},{1... | collective-permute-start | bytes 1572872 | tf_op jit(solution)/shard_map/ppermute | solution.py:453
  207.4 12.7 %collective-permute-start.30 = (f32[8,32,512]{2,1,0:T(8,128)S(1)}, f32[8,32,512]{2,1,0:T(8,128)S(1)}, u32[]{:S(2)}, u32[]{:S(2)}) collective-permute-start(f32[8,32,512]{2,1,0:T(8,128)S(1)} %get-tuple-element.122), channel_id=1, source_target_pairs={{0,1},{1,2},{2,3},{3,0},{4,5},{5,6},{6,7},{7,4},{8,9},{9,10},{10,1... | collective-permute-start | bytes 1572872 | tf_op jit(solution)/shard_map/ppermute | solution.py:453
  207.6 12.5 %collective-permute-start.31 = (f32[8,32,512]{2,1,0:T(8,128)S(1)}, f32[8,32,512]{2,1,0:T(8,128)S(1)}, u32[]{:S(2)}, u32[]{:S(2)}) collective-permute-start(f32[8,32,512]{2,1,0:T(8,128)S(1)} %get-tuple-element.124), channel_id=1, source_target_pairs={{0,3},{1,0},{2,1},{3,2},{4,7},{5,4},{6,5},{7,6},{8,11},{9,8},{10,9... | collective-permute-start | bytes 1572872 | tf_op jit(solution)/shard_map/ppermute | solution.py:453
  220.5 6.5 %collective-permute-start.32 = (f32[4,32,512]{2,1,0:T(8,128)S(1)}, f32[4,32,512]{2,1,0:T(8,128)S(1)}, u32[]{:S(2)}, u32[]{:S(2)}) collective-permute-start(f32[4,32,512]{2,1,0:T(8,128)S(1)} %get-tuple-element.126), channel_id=1, source_target_pairs={{0,1},{1,2},{2,3},{3,0},{4,5},{5,6},{6,7},{7,4},{8,9},{9,10},{10,1... | collective-permute-start | bytes 786440 | tf_op jit(solution)/shard_map/ppermute | solution.py:372
  221.2 7.4 %collective-permute-start.33 = (f32[4,32,512]{2,1,0:T(8,128)S(1)}, f32[4,32,512]{2,1,0:T(8,128)S(1)}, u32[]{:S(2)}, u32[]{:S(2)}) collective-permute-start(f32[4,32,512]{2,1,0:T(8,128)S(1)} %get-tuple-element.127), channel_id=1, source_target_pairs={{0,3},{1,0},{2,1},{3,2},{4,7},{5,4},{6,5},{7,6},{8,11},{9,8},{10,9... | collective-permute-start | bytes 786440 | tf_op jit(solution)/shard_map/ppermute | solution.py:373
  223.2 9.8 %collective-permute-start.34 = (f32[4,32,512]{2,1,0:T(8,128)S(1)}, f32[4,32,512]{2,1,0:T(8,128)S(1)}, u32[]{:S(2)}, u32[]{:S(2)}) collective-permute-start(f32[4,32,512]{2,1,0:T(8,128)S(1)} %get-tuple-element.128), channel_id=1, source_target_pairs={{0,2},{1,3},{2,0},{3,1},{4,6},{5,7},{6,4},{7,5},{8,10},{9,11},{10,... | collective-permute-start | bytes 786440 | tf_op jit(solution)/shard_map/ppermute | solution.py:371
  224.1 9.1 %collective-permute-start.35 = (f32[4,32,512]{2,1,0:T(8,128)S(1)}, f32[4,32,512]{2,1,0:T(8,128)S(1)}, u32[]{:S(2)}, u32[]{:S(2)}) collective-permute-start(f32[4,32,512]{2,1,0:T(8,128)S(1)} %get-tuple-element.130), channel_id=1, source_target_pairs={{0,4},{1,5},{2,6},{3,7},{4,8},{5,9},{6,10},{7,11},{8,12},{9,13},{1... | collective-permute-start | bytes 786440 | tf_op jit(solution)/shard_map/ppermute | solution.py:372
  224.3 29.2 %collective-permute-start.21 = (f32[512,256]{1,0:T(8,128)S(1)}, f32[512,256]{1,0:T(8,128)S(1)}, u32[]{:S(2)}, u32[]{:S(2)}) collective-permute-start(f32[512,256]{1,0:T(8,128)S(1)} %get-tuple-element.143), channel_id=1, source_target_pairs={{0,64},{16,80},{32,96},{48,112},{64,0},{80,16},{96,32},{112,48},{1... | collective-permute-start | bytes 1572872 | tf_op jit(solution)/shard_map/ppermute | solution.py:448
  227.0 30.6 %collective-permute-start.22 = (f32[512,256]{1,0:T(8,128)S(1)}, f32[512,256]{1,0:T(8,128)S(1)}, u32[]{:S(2)}, u32[]{:S(2)}) collective-permute-start(f32[512,256]{1,0:T(8,128)S(1)} %get-tuple-element.142), channel_id=1, source_target_pairs={{0,32},{16,48},{32,64},{48,80},{64,96},{80,112},{96,0},{112,16},{1... | collective-permute-start | bytes 1572872 | tf_op jit(solution)/shard_map/ppermute | solution.py:448
  228.6 29.8 %collective-permute-start.23 = (f32[512,256]{1,0:T(8,128)S(1)}, f32[512,256]{1,0:T(8,128)S(1)}, u32[]{:S(2)}, u32[]{:S(2)}) collective-permute-start(f32[512,256]{1,0:T(8,128)S(1)} %get-tuple-element.141), channel_id=1, source_target_pairs={{0,96},{16,112},{32,0},{48,16},{64,32},{80,48},{96,64},{112,80},{1... | collective-permute-start | bytes 1572872 | tf_op jit(solution)/shard_map/ppermute | solution.py:448
  233.0 5.5 %collective-permute-start.36 = (f32[4,32,512]{2,1,0:T(8,128)S(1)}, f32[4,32,512]{2,1,0:T(8,128)S(1)}, u32[]{:S(2)}, u32[]{:S(2)}) collective-permute-start(f32[4,32,512]{2,1,0:T(8,128)S(1)} %get-tuple-element.131), channel_id=1, source_target_pairs={{0,12},{1,13},{2,14},{3,15},{4,0},{5,1},{6,2},{7,3},{8,4},{9,5},{1... | collective-permute-start | bytes 786440 | tf_op jit(solution)/shard_map/ppermute | solution.py:373
  233.2 7.0 %collective-permute-start.37 = (f32[4,32,512]{2,1,0:T(8,128)S(1)}, f32[4,32,512]{2,1,0:T(8,128)S(1)}, u32[]{:S(2)}, u32[]{:S(2)}) collective-permute-start(f32[4,32,512]{2,1,0:T(8,128)S(1)} %get-tuple-element.132), channel_id=1, source_target_pairs={{0,8},{1,9},{2,10},{3,11},{4,12},{5,13},{6,14},{7,15},{8,0},{9,1},... | collective-permute-start | bytes 786440 | tf_op jit(solution)/shard_map/ppermute | solution.py:371
  241.6 7.9 %collective-permute-start.38 = (f32[32,512]{1,0:T(8,128)S(1)}, f32[32,512]{1,0:T(8,128)S(1)}, u32[]{:S(2)}, u32[]{:S(2)}) collective-permute-start(f32[32,512]{1,0:T(8,128)S(1)} %get-tuple-element.134), channel_id=1, source_target_pairs={{0,16},{16,0},{32,48},{48,32},{64,80},{80,64},{96,112},{112,96},{1... | collective-permute-start | bytes 196616 | tf_op jit(solution)/shard_map/ppermute | solution.py:461
  248.6 4.9 %collective-permute-start.39 = (f32[32,512]{1,0:T(8,128)S(1)}, f32[32,512]{1,0:T(8,128)S(1)}, u32[]{:S(2)}, u32[]{:S(2)}) collective-permute-start(f32[32,512]{1,0:T(8,128)S(1)} %get-tuple-element.135), channel_id=1, source_target_pairs={{0,32},{16,48},{32,64},{48,80},{64,96},{80,112},{96,0},{112,16},{1... | collective-permute-start | bytes 196616 | tf_op jit(solution)/shard_map/ppermute | solution.py:461
  249.5 12.5 %collective-permute-start.40 = (f32[32,512]{1,0:T(8,128)}, f32[32,512]{1,0:T(8,128)S(1)}, u32[]{:S(2)}, u32[]{:S(2)}) collective-permute-start(f32[32,512]{1,0:T(8,128)} %get-tuple-element.136), channel_id=1, source_target_pairs={{0,48},{16,32},{32,80},{48,64},{64,112},{80,96},{96,16},{112,0},{1... | collective-permute-start | bytes 196616 | tf_op jit(solution)/shard_map/ppermute | solution.py:461
  253.5 8.6 %collective-permute-start.41 = (f32[32,512]{1,0:T(8,128)}, f32[32,512]{1,0:T(8,128)S(1)}, u32[]{:S(2)}, u32[]{:S(2)}) collective-permute-start(f32[32,512]{1,0:T(8,128)} %get-tuple-element.137), channel_id=1, source_target_pairs={{0,64},{16,80},{32,96},{48,112},{64,0},{80,16},{96,32},{112,48},{1... | collective-permute-start | bytes 196616 | tf_op jit(solution)/shard_map/ppermute | solution.py:461
  253.5 8.6 %collective-permute-start.42 = (f32[32,512]{1,0:T(8,128)}, f32[32,512]{1,0:T(8,128)S(1)}, u32[]{:S(2)}, u32[]{:S(2)}) collective-permute-start(f32[32,512]{1,0:T(8,128)} %get-tuple-element.138), channel_id=1, source_target_pairs={{0,80},{16,64},{32,112},{48,96},{64,16},{80,0},{96,48},{112,32},{1... | collective-permute-start | bytes 196616 | tf_op jit(solution)/shard_map/ppermute | solution.py:461
  258.3 4.0 %collective-permute-start.43 = (f32[32,512]{1,0:T(8,128)}, f32[32,512]{1,0:T(8,128)}, u32[]{:S(2)}, u32[]{:S(2)}) collective-permute-start(f32[32,512]{1,0:T(8,128)} %get-tuple-element.139), channel_id=1, source_target_pairs={{0,96},{16,112},{32,0},{48,16},{64,32},{80,48},{96,64},{112,80},{1... | collective-permute-start | bytes 196616 | tf_op jit(solution)/shard_map/ppermute | solution.py:461
  259.2 4.4 %collective-permute-start.44 = (f32[32,512]{1,0:T(8,128)}, f32[32,512]{1,0:T(8,128)}, u32[]{:S(2)}, u32[]{:S(2)}) collective-permute-start(f32[32,512]{1,0:T(8,128)} %get-tuple-element.140), channel_id=1, source_target_pairs={{0,112},{16,96},{32,16},{48,0},{64,48},{80,32},{96,80},{112,64},{1... | collective-permute-start | bytes 196616 | tf_op jit(solution)/shard_map/ppermute | solution.py:461
  (32 other events, 288.2 us)
